TPU v7x, 256 devices: a whole 4x4x8 slice. The times are simulated.
256 devices in a mesh: doc: 16 (over z_hi, x, core), vocab: 16 (over z_lo, y).
Axes of the slice: x: 4, y: 4, z: 8 (z_hi: 2, z_lo: 4; z = z_hi * 4 + z_lo), core: 2. Of those that a mesh axis runs over, the one named last changes fastest.
Arguments:
- counts: bfloat16 [1024, 512, 128], P('doc', 'vocab'), may hold values from 0.099609375 to 3
- tile_index: int32 [1024, 512], P('doc', 'vocab'), may hold values from 0 to 31
- tile_count: int32 [1024, 256], P('doc', 'vocab'), may hold values from 0 to 2
- whitening: bfloat16 [1048576, 512], P(('doc', 'vocab')), may hold values from -0.046875 to 0.046875
- factors: float32 [512, 512], replicated, may hold values from -6 to 6
Outputs:
- gradient: float32 [512, 512], replicated
Inputs may be any that keep to these rules, and one draw needn't show every extreme that they name: `tile_count`: slots at or past a document block's live count carry no data. `tile_index`: tile numbers within a row block; two live slots may name the same tile.
All inputs are finite; a program needn't handle non-finite values.
Results may differ from a plain program's by a relative error of at most 0.00033.
Values may be sent and summed in bfloat16 or wider, within the bound.
No kernel may reach another device: no remote copies, remote signals or barrier semaphores. Data moves between devices by JAX's collectives and lax.ppermute only.
A program may use at most 64 MiB of HBM per device.

v0:
```python
import math

import jax
import jax.numpy as jnp
from jax import lax
from jax.sharding import PartitionSpec as P

penalty = 0.25


def project_rows(tile_rows, slot_tile, whitening, row_count):
    tile_width = tile_rows.shape[2]
    tiles_block = whitening.shape[0] // tile_width
    topics = whitening.shape[1]
    tile_iota = lax.broadcasted_iota(jnp.int32, (1, 1, tiles_block), 2)

    def one_group(inputs):
        group_counts, group_index = inputs
        onehot = (group_index[:, :, None] == tile_iota).astype(jnp.bfloat16)
        dense_block = jnp.einsum(
            "dst,dsw->dtw", onehot, group_counts, preferred_element_type=jnp.float32
        )
        dense_block = dense_block.astype(jnp.bfloat16).reshape(
            group_counts.shape[0], tiles_block * tile_width
        )
        return jnp.dot(dense_block, whitening, preferred_element_type=jnp.float32)

    groups = row_count // 512
    grouped = (
        tile_rows.reshape((groups, 512) + tile_rows.shape[1:]),
        slot_tile.reshape(groups, 512, slot_tile.shape[1]),
    )
    return lax.map(one_group, grouped).reshape(row_count, topics)


def shards(counts, tile_index, tile_count, whitening, factors):
    doc_devices = lax.axis_size("doc")
    doc_local = counts.shape[0]
    slot_count = counts.shape[1] // doc_devices
    tile_width = counts.shape[2]
    topics = whitening.shape[1]
    doc_total = doc_local * doc_devices
    slot_iota = lax.broadcasted_iota(jnp.int32, (1, 1, slot_count), 2)
    live_slot = slot_iota < tile_count[:, :, None]
    masked = jnp.where(
        live_slot[:, :, :, None],
        counts.reshape(doc_local, doc_devices, slot_count, tile_width),
        jnp.zeros((), jnp.bfloat16),
    )
    marked = jnp.where(live_slot, tile_index.reshape(doc_local, doc_devices, slot_count), -1)
    moved_counts, moved_index = (
        lax.all_to_all(masked, "doc", split_axis=1, concat_axis=0, tiled=True),
        lax.all_to_all(marked, "doc", split_axis=1, concat_axis=0, tiled=True),
    )
    tile_rows = moved_counts.reshape(doc_total, slot_count, tile_width)
    slot_tile = moved_index.reshape(doc_total, slot_count)
    all_terms = project_rows(tile_rows, slot_tile, whitening, doc_total)
    projected = lax.psum_scatter(all_terms, ("doc", "vocab"), scatter_dimension=0, tiled=True)
    highest = lax.Precision.HIGHEST
    inverse_root = 1.0 / math.sqrt(topics)
    scores = jnp.dot(projected, factors, precision=highest) * inverse_root
    local_moment = jnp.dot(projected.T, scores * scores, precision=highest)
    moment_total = lax.psum(local_moment, ("doc", "vocab"))
    moment = moment_total / doc_total
    gram_matrix = jnp.dot(factors.T, factors, precision=highest) / topics
    return moment - penalty * jnp.dot(factors, gram_matrix * gram_matrix, precision=highest)


def solution(mesh):
    in_specs = (
        P("doc", "vocab", None),
        P("doc", "vocab"),
        P("doc", "vocab"),
        P(("doc", "vocab"), None),
        P(),
    )
    out_specs = P()
    return jax.shard_map(shards, mesh=mesh, in_specs=in_specs, out_specs=out_specs, check_vma=False)
```

profile of v0, /device:TPU:1, one launch (start us, length us, event | category | flops | bytes accessed | tf_op | source)
XLA Modules:
  0.0 601.4 jit_solution(6161637919981206358)
XLA Ops:
  6.5 0.0 copy-start
  6.5 0.8 fusion.26
  7.4 0.7 reshape.24
  8.0 12.4 %all-to-all-start = ((s32[16,1,128]{2,1,0:T(1,128)}), s32[16,1,128]{2,1,0:T(1,128)S(1)}, u32[]{:S(2)}, u32[]{:S(2)}) async-start(s32[16,1,128]{2,1,0:T(1,128)} %reshape.24), calls=%async_computation | async-start | bytes 16384 | tf_op jit(solution)/shard_map/all_to_all | solution.py:53
  20.5 0.7 iota_compare_fusion
  21.2 0.3 copy.13
  21.5 3.8 broadcast_select_fusion
  25.3 4.6 all-to-all-done
  29.9 5.1 all-to-all-start.1
  35.0 0.0 all-reduce.6.cloned.1.call-start
  35.0 0.5 broadcast.10
  35.5 0.6 reduce
  36.1 0.1 reshape.25
  36.2 0.2 copy.18
  36.4 13.4 %all-to-all-done.1 = bf16[64,16,2,128]{3,2,0,1:T(2,128)(2,1)S(1)} async-done(((bf16[64,16,2,128]{3,2,0,1:T(2,128)(2,1)}), bf16[64,16,2,128]{3,2,0,1:T(2,128)(2,1)S(1)}, u32[]{:S(2)}, u32[]{:S(2)}) %all-to-all-start.1) | async-done | bytes 524320 | tf_op jit(solution)/shard_map/all_to_all | solution.py:52
  49.9 14.8 %while.11 = (s32[]{:T(128)}, f32[2,512,512]{2,1,0:T(8,128)}, s32[2,512,2]{2,1,0:T(8,128)S(1)}, bf16[2,512,2,128]{3,2,1,0:T(2,128)(2,1)S(1)}, bf16[4096,512]{1,0:T(8,128)(2,1)}, /*index=5*/s32[]{:T(128)}) while((s32[]{:T(128)}, f32[2,512,512]{2,1,0:T(8,128)}, s32[2,512,2]{2,1,0:T(8,128)S(1)}, ...), condition=%wide.region_1.2_spmd.clone, body=%wide.region_0.1_spmd.clone.sunk | while | flops 2158002176 | bytes 30941800 | solution.py:33
  49.9 0.0 copy-start.1
  49.9 4.0 convolution_convert_fusion.2
  53.9 0.0 copy-done.1
  53.9 3.3 fusion.43
  57.2 0.0 copy-start.1
  57.2 4.0 convolution_convert_fusion.2
  61.3 3.4 fusion.43
  64.6 0.0 all-reduce.6.cloned.1.call-update
  64.6 0.0 all-reduce.4.cloned.1.call-start
  64.7 262.6 %all-reduce.6.cloned.1.call-done = f32[1024,512]{1,0:T(8,128)} async-done(((f32[1024,512]{1,0:T(8,128)}), f32[1024,512]{1,0:T(8,128)}) %all-reduce.6.cloned.1.call-update) | async-done | bytes 2097168
  327.3 1.3 fusion.20
  328.6 2.7 fusion.21
  331.3 0.0 all-reduce.4.cloned.1.call-update
  331.3 1.9 fusion.19
  333.2 257.3 %all-reduce.4.cloned.1.call-done = f32[512,512]{1,0:T(8,128)} async-done(((f32[512,512]{1,0:T(8,128)}), f32[512,512]{1,0:T(8,128)}) %all-reduce.4.cloned.1.call-update) | async-done | bytes 1048592 | tf_op jit(solution)/shard_map/psum | solution.py:63
  590.5 4.1 fusion.18
  (6 shorter events, 0.0 us)
Async XLA Ops:
  6.5 320.7 %copy-start = (f32[512,512]{1,0:T(8,128)S(1)}, f32[512,512]{1,0:T(8,128)}, u32[]{:S(2)}) copy-start(f32[512,512]{1,0:T(8,128)} %param.11) | copy-start | bytes 3145732
  8.0 21.9 %all-to-all-start = ((s32[16,1,128]{2,1,0:T(1,128)}), s32[16,1,128]{2,1,0:T(1,128)S(1)}, u32[]{:S(2)}, u32[]{:S(2)}) async-start(s32[16,1,128]{2,1,0:T(1,128)} %reshape.24), calls=%async_computation | async-start | bytes 16384 | tf_op jit(solution)/shard_map/all_to_all | solution.py:53
  29.9 20.0 %all-to-all-start.1 = ((bf16[64,16,2,128]{3,2,0,1:T(2,128)(2,1)}), bf16[64,16,2,128]{3,2,0,1:T(2,128)(2,1)S(1)}, u32[]{:S(2)}, u32[]{:S(2)}) async-start(bf16[64,16,2,128]{3,2,0,1:T(2,128)(2,1)} %broadcast_select_fusion), calls=%async_computation.1 | async-start | bytes 1048576 | tf_op jit(solution)/shard_map/all_to_all | solution.py:52
  35.0 292.3 %all-reduce.6.cloned.1.call-start = ((), (), s32[]{:S(2)}) async-start(), calls=%async_computation.3 | async-start | bytes 4194304
  49.9 4.0 copy-start.1
  57.2 4.0 copy-start.1
  64.6 525.8 %all-reduce.4.cloned.1.call-start = ((), (), s32[]{:S(2)}) async-start(), calls=%async_computation.2 | async-start | bytes 2097152 | tf_op jit(solution)/shard_map/psum | solution.py:63
Sparse Core Ops, SparseCore 0:
  64.8 262.4 all-reduce.5
  332.7 257.7 all-reduce.3
where the time goes:
time: 603 us; the launch traced here: 601 us
  waiting for transfers between devices  538 us (89%)
  matrix products  24.6 us (4%)
  starting transfers between devices  17.6 us (3%)
  between operations  13.5 us (2%)
    unnamed x3, waiting for transfers between devices  263 us
    psum x1, waiting for transfers between devices, shards(): moment_total = lax.psum(local_moment, ('doc', 'vocab'))  257 us
    all_to_all x1, waiting for transfers between devices, shards(): lax.all_to_all(masked, 'doc', split_axis=1, concat_axis=0, tiled=True)  13.4 us
    all_to_all x1, starting transfers between devices, shards(): lax.all_to_all(marked, 'doc', split_axis=1, concat_axis=0, tiled=True)  12.4 us
  transfers between devices with their start and end apart: 4, of which 4 were waited for; matrix products, arithmetic and copies ran while one was open for 1% of the time, Pallas kernels for 0%

commit v1 on v0

v1 whole, which is shorter than its diff:
```python
import math

import jax
import jax.numpy as jnp
from jax import lax
from jax.sharding import Mesh, PartitionSpec as P

penalty = 0.25
term_scale = 256.0
total_scale = 4.0
HIGH = lax.Precision.HIGH


def project_rows(tile_rows, slot_tile, whitening):
    rows, _, tile_width = tile_rows.shape
    tiles_block = whitening.shape[0] // tile_width
    tile_iota = lax.broadcasted_iota(jnp.int32, (1, 1, tiles_block), 2)
    onehot = (slot_tile[:, :, None] == tile_iota).astype(jnp.bfloat16)
    dense_block = jnp.einsum("dst,dsw->dtw", onehot, tile_rows, preferred_element_type=jnp.float32)
    dense_block = dense_block.astype(jnp.bfloat16).reshape(rows, tiles_block * tile_width)
    return jnp.dot(dense_block, whitening, preferred_element_type=jnp.float32)


def to_half(values, scale):
    return (values * scale).astype(jnp.float16)


def from_half(values, scale):
    return values.astype(jnp.float32) * (1.0 / scale)


def shards(counts, tile_index, tile_count, whitening, factors):
    doc_axes = ("zh", "x", "c")
    doc_devices = lax.axis_size(doc_axes)
    doc_local = counts.shape[0]
    slot_count = counts.shape[1] // doc_devices
    tile_width = counts.shape[2]
    topics = whitening.shape[1]
    doc_total = doc_local * doc_devices
    slot_iota = lax.broadcasted_iota(jnp.int32, (1, 1, slot_count), 2)
    live_slot = slot_iota < tile_count[:, :, None]
    marked = jnp.where(live_slot, tile_index.reshape(doc_local, doc_devices, slot_count), -1)
    blocks = counts.reshape(doc_local, doc_devices, slot_count, tile_width)
    moved_index = lax.all_to_all(marked, doc_axes, split_axis=1, concat_axis=0, tiled=True)
    moved_counts = lax.all_to_all(blocks, doc_axes, split_axis=1, concat_axis=0, tiled=True)
    tile_rows = moved_counts.reshape(doc_total, slot_count, tile_width)
    slot_tile = moved_index.reshape(doc_total, slot_count)
    terms = project_rows(tile_rows, slot_tile, whitening)

    core = lax.axis_index("c")
    half = doc_total // 2
    swap = [(0, 1), (1, 0)]
    away = lax.dynamic_slice_in_dim(terms, (1 - core) * half, half, 0)
    kept = lax.dynamic_slice_in_dim(terms, core * half, half, 0)
    kept = kept + from_half(lax.ppermute(to_half(away, term_scale), "c", swap), term_scale)

    plane = lax.axis_size(("x", "y"))
    column = lax.axis_size(("zh", "zl"))
    part = half // plane
    sent = to_half(kept, term_scale).reshape(plane, part, topics)
    got = lax.all_to_all(sent, ("x", "y"), 0, 0, tiled=True)
    plane_sum = jnp.sum(got.astype(jnp.float32), axis=0) * (1.0 / term_scale)
    sent = jnp.broadcast_to(to_half(plane_sum, total_scale)[None], (column, part, topics))
    got = lax.all_to_all(sent, ("zh", "zl"), 0, 0, tiled=True)
    total = jnp.sum(got.astype(jnp.float32), axis=0) * (1.0 / total_scale)
    sent = jnp.broadcast_to(to_half(total, total_scale)[None], (plane, part, topics))
    got = lax.all_to_all(sent, ("x", "y"), 0, 0, tiled=True)
    projected = from_half(got.reshape(half, topics), total_scale)

    scores = jnp.dot(projected, factors, precision=HIGH) * (1.0 / math.sqrt(topics))
    moment = jnp.dot(projected.T, scores * scores, precision=HIGH)
    moment = (moment + lax.ppermute(moment, "c", swap)) / doc_total
    gram_matrix = jnp.dot(factors.T, factors, precision=HIGH) / topics
    return moment - penalty * jnp.dot(factors, gram_matrix * gram_matrix, precision=HIGH)


def solution(mesh):
    fine = Mesh(mesh.devices.reshape(2, 4, 2, 4, 4), ("zh", "x", "c", "zl", "y"))
    doc, vocab = ("zh", "x", "c"), ("zl", "y")
    in_specs = (P(doc, vocab, None), P(doc, vocab), P(doc, vocab), P(doc + vocab, None), P())
    return jax.shard_map(shards, mesh=fine, in_specs=in_specs, out_specs=P(), check_vma=False)
```

time: 603 us -> 116 us (0.19)
  waiting for transfers between devices: 538 us -> 23.6 us
  blocking collectives: 0 us -> 44.5 us
  between operations: 13.5 us -> 0.12 us
  matrix products: 24.6 us -> 17.4 us
    unnamed x3 -> x0, waiting for transfers between devices: 263 us -> none
    psum x1 -> x0, waiting for transfers between devices: 257 us -> none  [shards(): moment_total = lax.psum(local_moment, ('doc', 'vocab'))]
    all_to_all x0 -> x3, blocking collectives: none -> 44.5 us  [the longest x2 28.5 us: shards(): got = lax.all_to_all(sent, ('x', 'y'), 0, 0, tiled=True)]
    dot_general x8 -> x6, matrix products: 24.6 us -> 17.4 us  [the longest x1 7.68 us: project_rows(): jnp.einsum('dst,dsw->dtw', onehot, tile_rows, preferred_element_type=jnp....]
  transfers between devices with their start and end apart: 4 -> 4, of which waited for: 4 -> 4; matrix products, arithmetic and copies ran while one was open for 1% -> 4% of each run, Pallas kernels for 0% -> 0%
where the time goes in v1:
time: 116 us; the launch traced here: 115 us
  blocking collectives  44.5 us (38%)
  waiting for transfers between devices  23.6 us (20%)
  starting transfers between devices  21.7 us (19%)
  matrix products  17.4 us (15%)
  local copies, waits for them, and re-layouts  4 us (3%)
  other arithmetic  3.99 us (3%)
    all_to_all x2, blocking collectives, shards(): got = lax.all_to_all(sent, ('x', 'y'), 0, 0, tiled=True)  28.5 us
    all_to_all x1, blocking collectives, shards(): got = lax.all_to_all(sent, ('zh', 'zl'), 0, 0, tiled=True)  16 us
    all_to_all x1, waiting for transfers between devices, shards(): lax.all_to_all(blocks, doc_axes, split_axis=1, concat_axis=0, tiled=True)  13.4 us
    all_to_all x1, starting transfers between devices, shards(): lax.all_to_all(marked, doc_axes, split_axis=1, concat_axis=0, tiled=True)  12.4 us
    dot_general x1, matrix products, project_rows(): jnp.einsum('dst,dsw->dtw', onehot, tile_rows, preferred_element_type=jnp....  7.68 us
    all_to_all x1, waiting for transfers between devices, shards(): lax.all_to_all(marked, doc_axes, split_axis=1, concat_axis=0, tiled=True)  7.1 us
    dot_general x1, matrix products, project_rows(): return jnp.dot(dense_block, whitening, preferred_element_type=jnp.float32)  4.5 us
    ppermute x1, starting transfers between devices, shards(): moment = (moment + lax.ppermute(moment, 'c', swap)) / doc_total  4.21 us
  transfers between devices with their start and end apart: 4, of which 4 were waited for; matrix products, arithmetic and copies ran while one was open for 4% of the time, Pallas kernels for 0%

profile of v1, /device:TPU:1, one launch (start us, length us, event | category | flops | bytes accessed | tf_op | source)
XLA Modules:
  0.0 115.2 jit_solution(7137340230956082897)
XLA Ops:
  0.0 0.0 copy-start
  0.0 0.8 fusion.9
  0.8 0.7 reshape.35
  1.5 12.4 %all-to-all-start = ((s32[16,1,128]{2,1,0:T(1,128)}), s32[16,1,128]{2,1,0:T(1,128)S(1)}, u32[]{:S(2)}, u32[]{:S(2)}) async-start(s32[16,1,128]{2,1,0:T(1,128)} %reshape.35), calls=%async_computation | async-start | bytes 16384 | tf_op jit(solution)/shard_map/all_to_all | solution.py:44
  13.9 2.3 %copy.18 = bf16[64,16,2,128]{3,2,0,1:T(2,128)(2,1)} copy(bf16[64,16,2,128]{3,2,1,0:T(2,128)(2,1)} %bitcast.42) | data formatting | bytes 1048576 | tf_op jit(solution)/shard_map/reshape | solution.py:43
  16.3 7.1 %all-to-all-done = s32[16,1,128]{2,1,0:T(1,128)S(1)} async-done(((s32[16,1,128]{2,1,0:T(1,128)}), s32[16,1,128]{2,1,0:T(1,128)S(1)}, u32[]{:S(2)}, u32[]{:S(2)}) %all-to-all-start) | async-done | bytes 8224 | tf_op jit(solution)/shard_map/all_to_all | solution.py:44
  23.4 3.9 %all-to-all-start.1 = ((bf16[64,16,2,128]{3,2,0,1:T(2,128)(2,1)}), bf16[64,16,2,128]{3,2,0,1:T(2,128)(2,1)S(1)}, u32[]{:S(2)}, u32[]{:S(2)}) async-start(bf16[64,16,2,128]{3,2,0,1:T(2,128)(2,1)} %copy.18), calls=%async_computation.1 | async-start | bytes 1048576 | tf_op jit(solution)/shard_map/all_to_all | solution.py:45
  27.2 0.6 broadcast.33
  27.8 0.7 reduce
  28.5 0.1 reshape.36
  28.6 0.2 copy.21
  28.9 13.4 %all-to-all-done.1 = bf16[64,16,2,128]{3,2,0,1:T(2,128)(2,1)S(1)} async-done(((bf16[64,16,2,128]{3,2,0,1:T(2,128)(2,1)}), bf16[64,16,2,128]{3,2,0,1:T(2,128)(2,1)S(1)}, u32[]{:S(2)}, u32[]{:S(2)}) %all-to-all-start.1) | async-done | bytes 524320 | tf_op jit(solution)/shard_map/all_to_all | solution.py:45
  42.3 0.0 copy-start.1
  42.3 7.7 %convolution_convert_fusion = bf16[1024,32,128]{2,1,0:T(8,128)(2,1)S(1)} fusion(bf16[1024,2,128]{2,1,0:T(2,128)(2,1)S(1)} %bitcast.39, s32[1024,2]{1,0:T(8,128)S(1)} %bitcast.40), kind=kOutput, calls=%fused_computation.3 | convolution fusion | flops 21037056 | bytes 8921088 | tf_op jit(solution)/shard_map/dst,dsw->dtw/dot_general | solution.py:19
  49.9 0.0 copy-done.1
  50.0 4.5 %fusion = f32[1024,512]{1,0:T(8,128)S(1)} fusion(bf16[4096,512]{1,0:T(8,128)(2,1)S(1)} %copy-done.1, bf16[128,8,32,128]{3,2,1,0:T(8,128)(2,1)S(1)} %bitcast.38), kind=kOutput, calls=%fused_computation | convolution fusion | flops 4294967296 | bytes 14680064 | tf_op jit(solution)/shard_map/dot_general | solution.py:21
  54.5 0.9 multiply_convert_fusion.1
  55.4 1.2 %collective-permute-start = (f16[512,512]{1,0:T(8,128)(2,1)}, f16[512,512]{1,0:T(8,128)(2,1)}, u32[]{:S(2)}, u32[]{:S(2)}) collective-permute-start(f16[512,512]{1,0:T(8,128)(2,1)} %multiply_convert_fusion.1), channel_id=1, source_target_pairs={{0,16},{16,0},{1,17},{17,1},{2,18},{18,2},{3,19},{19,3},{4,20},{20... | collective-permute-start | bytes 1572872 | tf_op jit(solution)/shard_map/ppermute | solution.py:55
  56.6 1.9 %collective-permute-done = f16[512,512]{1,0:T(8,128)(2,1)} collective-permute-done((f16[512,512]{1,0:T(8,128)(2,1)}, f16[512,512]{1,0:T(8,128)(2,1)}, u32[]{:S(2)}, u32[]{:S(2)}) %collective-permute-start) | collective-permute-done | bytes 524320 | tf_op jit(solution)/shard_map/ppermute | solution.py:55
  58.5 1.2 %multiply_convert_fusion = f16[512,512]{1,0:T(8,128)(2,1)S(1)} fusion(f16[512,512]{1,0:T(8,128)(2,1)} %collective-permute-done, f32[1024,512]{1,0:T(8,128)S(1)} %fusion, s32[]{:T(128)S(6)} %select_n.11), kind=kLoop, calls=%fused_computation.14 | loop fusion | flops 1310720 | bytes 2097156 | tf_op jit(solution)/shard_map/convert_element_type | solution.py:25
  59.7 14.8 %all_to_all.45 = f16[16,32,512]{2,1,0:T(8,128)(2,1)S(1)} all-to-all(f16[16,32,512]{2,1,0:T(8,128)(2,1)S(1)} %bitcast.41), channel_id=1, replica_groups=mesh['zh'=2,'x'=4,'c'=2,'zl'=4,'y'=4] {'x','y'}, dimensions={0} | all-to-all | bytes 1048576 | tf_op jit(solution)/shard_map/all_to_all | solution.py:61
  74.6 0.1 convert_reduce_fusion
  74.7 16.0 %all_to_all.46 = f16[8,32,512]{2,1,0:T(8,128)(2,1)S(1)} all-to-all(f16[8,32,512]{2,1,0:T(8,128)(2,1)S(1)} %broadcast_in_dim.9), channel_id=1, replica_groups=mesh['zh'=2,'x'=4,'c'=2,'zl'=4,'y'=4] {'zh','zl'}, dimensions={0} | all-to-all | bytes 524288 | tf_op jit(solution)/shard_map/all_to_all | solution.py:64
  90.8 13.7 %all_to_all.47 = f16[16,32,512]{2,1,0:T(8,128)(2,1)S(1)} all-to-all(f16[16,32,512]{2,1,0:T(8,128)(2,1)S(1)} %broadcast_in_dim.10), channel_id=1, replica_groups=mesh['zh'=2,'x'=4,'c'=2,'zl'=4,'y'=4] {'x','y'}, dimensions={0} | all-to-all | bytes 1048576 | tf_op jit(solution)/shard_map/all_to_all | solution.py:67
  104.4 0.1 convert_multiply_fusion
  104.6 0.0 copy-done
  104.6 1.0 fusion.6
  105.6 1.1 fusion.10
  106.7 4.2 %collective-permute-start.1 = (f32[512,512]{1,0:T(8,128)S(1)}, f32[512,512]{1,0:T(8,128)S(1)}, u32[]{:S(2)}, u32[]{:S(2)}) collective-permute-start(f32[512,512]{1,0:T(8,128)S(1)} %fusion.10), channel_id=1, source_target_pairs={{0,16},{16,0},{1,17},{17,1},{2,18},{18,2},{3,19},{19,3},{4,20},{20... | collective-permute-start | bytes 3145736 | tf_op jit(solution)/shard_map/ppermute | solution.py:72
  110.9 1.0 fusion.5
  111.9 1.2 %collective-permute-done.1 = f32[512,512]{1,0:T(8,128)S(1)} collective-permute-done((f32[512,512]{1,0:T(8,128)S(1)}, f32[512,512]{1,0:T(8,128)S(1)}, u32[]{:S(2)}, u32[]{:S(2)}) %collective-permute-start.1) | collective-permute-done | bytes 1048608 | tf_op jit(solution)/shard_map/ppermute | solution.py:72
  113.2 2.1 %multiply_subtract_fusion = f32[512,512]{1,0:T(8,128)} fusion(f32[512,512]{1,0:T(8,128)S(1)} %fusion.10, f32[512,512]{1,0:T(8,128)S(1)} %collective-permute-done.1, f32[512,512]{1,0:T(8,128)S(1)} %fusion.5, f32[512,512]{1,0:T(8,128)S(1)} %copy-done), kind=kOutput, calls=%fused_computation.11 | convolution fusion | flops 806354944 | bytes 5242880 | tf_op jit(solution)/shard_map/dot_general | solution.py:74
  (6 shorter events, 0.1 us)
Async XLA Ops:
  0.0 104.6 %copy-start = (f32[512,512]{1,0:T(8,128)S(1)}, f32[512,512]{1,0:T(8,128)}, u32[]{:S(2)}) copy-start(f32[512,512]{1,0:T(8,128)} %param.9) | copy-start | bytes 3145732
  1.5 21.8 %all-to-all-start = ((s32[16,1,128]{2,1,0:T(1,128)}), s32[16,1,128]{2,1,0:T(1,128)S(1)}, u32[]{:S(2)}, u32[]{:S(2)}) async-start(s32[16,1,128]{2,1,0:T(1,128)} %reshape.35), calls=%async_computation | async-start | bytes 16384 | tf_op jit(solution)/shard_map/all_to_all | solution.py:44
  23.4 18.9 %all-to-all-start.1 = ((bf16[64,16,2,128]{3,2,0,1:T(2,128)(2,1)}), bf16[64,16,2,128]{3,2,0,1:T(2,128)(2,1)S(1)}, u32[]{:S(2)}, u32[]{:S(2)}) async-start(bf16[64,16,2,128]{3,2,0,1:T(2,128)(2,1)} %copy.18), calls=%async_computation.1 | async-start | bytes 1048576 | tf_op jit(solution)/shard_map/all_to_all | solution.py:45
  42.3 7.7 %copy-start.1 = (bf16[4096,512]{1,0:T(8,128)(2,1)S(1)}, bf16[4096,512]{1,0:T(8,128)(2,1)}, u32[]{:S(2)}) copy-start(bf16[4096,512]{1,0:T(8,128)(2,1)} %param.8) | copy-start | bytes 12582916
  55.4 3.1 %collective-permute-start = (f16[512,512]{1,0:T(8,128)(2,1)}, f16[512,512]{1,0:T(8,128)(2,1)}, u32[]{:S(2)}, u32[]{:S(2)}) collective-permute-start(f16[512,512]{1,0:T(8,128)(2,1)} %multiply_convert_fusion.1), channel_id=1, source_target_pairs={{0,16},{16,0},{1,17},{17,1},{2,18},{18,2},{3,19},{19,3},{4,20},{20... | collective-permute-start | bytes 1572872 | tf_op jit(solution)/shard_map/ppermute | solution.py:55
  106.7 6.5 %collective-permute-start.1 = (f32[512,512]{1,0:T(8,128)S(1)}, f32[512,512]{1,0:T(8,128)S(1)}, u32[]{:S(2)}, u32[]{:S(2)}) collective-permute-start(f32[512,512]{1,0:T(8,128)S(1)} %fusion.10), channel_id=1, source_target_pairs={{0,16},{16,0},{1,17},{17,1},{2,18},{18,2},{3,19},{19,3},{4,20},{20... | collective-permute-start | bytes 3145736 | tf_op jit(solution)/shard_map/ppermute | solution.py:72

commit v2 on v1

v2 whole, which is shorter than its diff:
```python
import functools
import math

import jax
import jax.numpy as jnp
from jax import lax
from jax.experimental import pallas as pl
from jax.experimental.pallas import tpu as pltpu
from jax.sharding import Mesh, PartitionSpec as P

penalty = 0.25
term_scale = 256.0
total_scale = 4.0
HIGH = lax.Precision.HIGH
STEPS = 4


def pack_kernel(index_ref, live_ref, counts_ref, out_ref, sems):
    targets, units, group, width = out_ref.shape
    chips = targets // 2
    docs = units - 2
    copies = []
    for chip in range(chips):
        for core in range(2):
            target = chip * 2 + core
            copy = pltpu.make_async_copy(
                counts_ref.at[pl.ds(core * docs, docs), chip],
                out_ref.at[target, pl.ds(0, docs)],
                sems.at[target],
            )
            copy.start()
            copies.append(copy)
    slots = group // 2
    marked = []
    for lane in range(group):
        tile = index_ref[pl.ds(lane, chips, stride=group), :]
        live = live_ref[pl.ds(lane // slots, chips, stride=2), :]
        marked.append(jnp.where(lane % slots < live, tile, -1).astype(jnp.float32))
    for core in range(2):
        rows = jnp.concatenate([m[:, core * docs:(core + 1) * docs] for m in marked], axis=1)
        for chip in range(chips):
            row = jnp.broadcast_to(rows[chip:chip + 1, :], (2 * group, width))
            out_ref[chip * 2 + core, docs:docs + 2] = row.reshape(2, group, width).astype(out_ref.dtype)
    for copy in copies:
        copy.wait()


def project_kernel(core_ref, moved_ref, own_ref, other_ref, early_ref, out_ref,
                   weights, spread, values, tiles, sems):
    sources, rows, width = moved_ref.shape
    group = 4
    data = rows - 2 * group
    docs = data // group
    depth = own_ref.shape[0] // STEPS
    copies = []
    for step in range(2 * STEPS):
        source = own_ref if step < STEPS else other_ref
        copy = pltpu.make_async_copy(
            source.at[pl.ds((step % STEPS) * depth, depth)], weights.at[step], sems.at[step])
        copy.start()
        copies.append(copy)

    sub = lax.broadcasted_iota(jnp.int32, (8, width), 0)
    halves = []
    for base in range(0, sources, 8):
        part = jnp.zeros((8, width), jnp.float32)
        for k in range(8):
            part = jnp.where(sub == k, moved_ref[base + k, data:data + 8, :].astype(jnp.float32), part)
        halves.append(part)
    halves.append(jnp.zeros((width - sources, width), jnp.float32))
    index = jnp.transpose(jnp.concatenate(halves, axis=0))
    for k in range(sources):
        spread[k * data:(k + 1) * data, :] = moved_ref[k, :data, :].astype(jnp.float32)
    total = sources * docs
    for block in range(2):
        where = []
        for slot in range(2):
            lane = block * 2 + slot
            where.append(jnp.concatenate(
                [jnp.broadcast_to(index[lane * docs:(lane + 1) * docs, k:k + 1], (docs, width))
                 for k in range(sources)], axis=0))
        first = spread[pl.ds(block * 2, total, stride=group), :]
        second = spread[pl.ds(block * 2 + 1, total, stride=group), :]
        first = jnp.where(where[0] == where[1], first + second, first)
        values[block * 2] = first.astype(jnp.bfloat16)
        values[block * 2 + 1] = second.astype(jnp.bfloat16)
        tiles[block * 2] = where[0].astype(jnp.bfloat16)
        tiles[block * 2 + 1] = where[1].astype(jnp.bfloat16)

    core = core_ref[0]
    tiles_step = depth // width

    def one_step(step):
        block = jnp.where(step < STEPS, core, 1 - core)
        base = (lax.rem(step, STEPS) * tiles_step).astype(jnp.float32)
        base = jnp.full((1, width), base, jnp.float32).astype(jnp.bfloat16)
        tile_a = tiles[block * 2] - base
        tile_b = tiles[block * 2 + 1] - base
        value_a = values[block * 2]
        value_b = values[block * 2 + 1]
        none = jnp.zeros_like(value_a)
        parts = []
        for t in range(tiles_step):
            mark = jnp.full((1, width), t, jnp.bfloat16)
            parts.append(jnp.where(tile_a == mark, value_a, jnp.where(tile_b == mark, value_b, none)))
        dense = jnp.concatenate(parts, axis=1)
        pltpu.make_async_copy(own_ref.at[pl.ds(0, depth)], weights.at[step], sems.at[step]).wait()
        return jnp.dot(dense, weights[step], preferred_element_type=jnp.float32)

    out_ref[...] = one_step(jnp.int32(0))

    @pl.loop(1, 2 * STEPS)
    def _(step):
        out_ref[...] += one_step(step)


def to_half(values, scale):
    return (values * scale).astype(jnp.float16)


def from_half(values, scale):
    return values.astype(jnp.float32) * (1.0 / scale)


def shards(counts, tile_index, tile_count, whitening, factors):
    doc_axes = ("zh", "x", "c")
    doc_devices = lax.axis_size(doc_axes)
    chips = doc_devices // 2
    doc_local = counts.shape[0]
    slots = counts.shape[1] // doc_devices
    width = counts.shape[2]
    topics = whitening.shape[1]
    half = doc_local * chips
    group = 2 * slots
    swap = [(0, 1), (1, 0)]
    vmem = pl.BlockSpec(memory_space=pltpu.VMEM)
    anywhere = pl.BlockSpec(memory_space=pl.ANY)

    other = lax.ppermute(whitening, "c", swap)
    units = doc_local // 2 + 2
    packed = pl.pallas_call(
        pack_kernel,
        out_shape=jax.ShapeDtypeStruct((doc_devices, units, group, width), jnp.bfloat16),
        in_specs=[vmem, vmem, anywhere],
        out_specs=vmem,
        scratch_shapes=[pltpu.SemaphoreType.DMA((doc_devices,))],
        compiler_params=pltpu.CompilerParams(vmem_limit_bytes=8 << 20),
        cost_estimate=pl.CostEstimate(flops=1 << 20, bytes_accessed=2 << 20, transcendentals=0),
        name="pack",
    )(tile_index.T, tile_count.T, counts.reshape(doc_local, chips, group, width))
    moved = lax.all_to_all(packed, doc_axes, 0, 0, tiled=True)
    moved = moved.reshape(doc_devices, units * group, width)

    gram_matrix = jnp.dot(factors.T, factors, precision=HIGH) / topics
    early = penalty * jnp.dot(factors, gram_matrix * gram_matrix, precision=HIGH)
    core = lax.axis_index("c")
    depth = whitening.shape[0] // STEPS
    terms = pl.pallas_call(
        project_kernel,
        out_shape=jax.ShapeDtypeStruct((half, topics), jnp.float32),
        in_specs=[pl.BlockSpec(memory_space=pltpu.SMEM), vmem, anywhere, anywhere, anywhere],
        out_specs=vmem,
        scratch_shapes=[
            pltpu.VMEM((2 * STEPS, depth, topics), jnp.bfloat16),
            pltpu.VMEM((half * group, width), jnp.float32),
            pltpu.VMEM((group, half, width), jnp.bfloat16),
            pltpu.VMEM((group, half, width), jnp.bfloat16),
            pltpu.SemaphoreType.DMA((2 * STEPS,)),
        ],
        compiler_params=pltpu.CompilerParams(vmem_limit_bytes=24 << 20),
        cost_estimate=pl.CostEstimate(
            flops=4 * half * whitening.shape[0] * topics, bytes_accessed=12 << 20, transcendentals=0),
        name="project",
    )(core.astype(jnp.int32).reshape(1), moved, whitening, other, early)

    plane_axes, column_axes = ("y", "x"), ("zh", "zl")
    plane = lax.axis_size(plane_axes)
    column = lax.axis_size(column_axes)
    part = half // plane
    sent = to_half(terms, term_scale).reshape(plane, part, topics)
    got = lax.all_to_all(sent, plane_axes, 0, 0, tiled=True)
    plane_sum = jnp.sum(got.astype(jnp.float32), axis=0) * (1.0 / term_scale)
    sent = jnp.broadcast_to(to_half(plane_sum, total_scale)[None], (column, part, topics))
    got = lax.all_to_all(sent, column_axes, 0, 0, tiled=True)
    total = jnp.sum(got.astype(jnp.float32), axis=0) * (1.0 / total_scale)
    sent = jnp.broadcast_to(to_half(total, total_scale)[None], (plane, part, topics))
    got = lax.all_to_all(sent, plane_axes, 0, 0, tiled=True)
    projected = from_half(got.reshape(half, topics), total_scale)

    scores = jnp.dot(projected, factors, precision=HIGH) * (1.0 / math.sqrt(topics))
    moment = jnp.dot(projected.T, scores * scores, precision=HIGH)
    return (moment + lax.ppermute(moment, "c", swap)) * (1.0 / (2 * half)) - early


def solution(mesh):
    fine = Mesh(mesh.devices.reshape(2, 4, 2, 4, 4), ("zh", "x", "c", "zl", "y"))
    doc, vocab = ("zh", "x", "c"), ("zl", "y")
    in_specs = (P(doc, vocab, None), P(doc, vocab), P(doc, vocab), P(doc + vocab, None), P())
    return jax.shard_map(shards, mesh=fine, in_specs=in_specs, out_specs=P(), check_vma=False)
```

time: 116 us -> 103 us (0.89)
  Pallas kernels: 0 us -> 14 us
  matrix products: 17.4 us -> 4.07 us
  waiting for transfers between devices: 23.6 us -> 15.5 us
  starting transfers between devices: 21.7 us -> 16.6 us
  other arithmetic: 3.99 us -> 1.74 us
  blocking collectives: 44.5 us -> 45.8 us
    pallas_call x0 -> x2, Pallas kernels: none -> 14 us  [the longest x1 12.8 us: shards(): pl.pallas_call(project_kernel, out_shape=jax.ShapeDtypeStruct((half, topi...]
    dot_general x2 -> x0, matrix products: 12.2 us -> none  [the longest x1 7.68 us: project_rows(): jnp.einsum('dst,dsw->dtw', onehot, tile_rows, preferred_element_type=jnp....]
    all_to_all x2 -> x1, waiting for transfers between devices: 20.5 us -> 13.2 us  [shards(): moved = lax.all_to_all(packed, doc_axes, 0, 0, tiled=True)]
    all_to_all x2 -> x1, starting transfers between devices: 16.3 us -> 9.36 us  [shards(): moved = lax.all_to_all(packed, doc_axes, 0, 0, tiled=True)]
    unnamed x6 -> x10, local copies, waits for them, and re-layouts: 0.77 us -> 4.65 us
    reshape x1 -> x0, local copies, waits for them, and re-layouts: 2.32 us -> none  [shards(): blocks = counts.reshape(doc_local, doc_devices, slot_count, tile_width)]
    convert_element_type x4 -> x3, other arithmetic: 2.2 us -> 0.15 us  [to_half(): return (values * scale).astype(jnp.float16)]
    ppermute x2, starting transfers between devices: 5.41 us -> 7.22 us  [the longest x1 4.02 us: shards(): lax.ppermute(moment, 'c', swap)]
  transfers between devices with their start and end apart: 4 -> 3, of which waited for: 4 -> 2; matrix products, arithmetic and copies ran while one was open for 4% -> 2% of each run, Pallas kernels for 0% -> 1%
where the time goes in v2:
time: 103 us; the launch traced here: 102 us
  blocking collectives  45.8 us (44%)
  starting transfers between devices  16.6 us (16%)
  waiting for transfers between devices  15.5 us (15%)
  Pallas kernels  14 us (14%)
  local copies, waits for them, and re-layouts  4.72 us (5%)
  matrix products  4.07 us (4%)
  other arithmetic  1.74 us (2%)
    all_to_all x2, blocking collectives, shards(): got = lax.all_to_all(sent, plane_axes, 0, 0, tiled=True)  29.3 us
    all_to_all x1, blocking collectives, shards(): got = lax.all_to_all(sent, column_axes, 0, 0, tiled=True)  16.4 us
    all_to_all x1, waiting for transfers between devices, shards(): moved = lax.all_to_all(packed, doc_axes, 0, 0, tiled=True)  13.2 us
    pallas_call x1, Pallas kernels, shards(): pl.pallas_call(project_kernel, out_shape=jax.ShapeDtypeStruct((half, topi...  12.8 us
    all_to_all x1, starting transfers between devices, shards(): moved = lax.all_to_all(packed, doc_axes, 0, 0, tiled=True)  9.36 us
    unnamed x10, local copies, waits for them, and re-layouts  4.65 us
    ppermute x1, starting transfers between devices, shards(): lax.ppermute(moment, 'c', swap)  4.02 us
    ppermute x1, starting transfers between devices, shards(): other = lax.ppermute(whitening, 'c', swap)  3.2 us
  transfers between devices with their start and end apart: 3, of which 2 were waited for; matrix products, arithmetic and copies ran while one was open for 2% of the time, Pallas kernels for 1%

profile of v2, /device:TPU:1, one launch (start us, length us, event | category | flops | bytes accessed | tf_op | source)
XLA Modules:
  0.0 102.5 jit_solution(14095794182751751984)
XLA Ops:
  0.0 0.0 copy-start
  0.0 3.2 %collective-permute-start = (bf16[4096,512]{1,0:T(8,128)(2,1)}, bf16[4096,512]{1,0:T(8,128)(2,1)}, u32[]{:S(2)}, u32[]{:S(2)}) collective-permute-start(bf16[4096,512]{1,0:T(8,128)(2,1)} %own_ref.1), channel_id=1, source_target_pairs={{0,16},{16,0},{1,17},{17,1},{2,18},{18,2},{3,19},{19,3},{4,20},{20... | collective-permute-start | bytes 12582920 | tf_op jit(solution)/shard_map/ppermute | solution.py:139
  3.2 0.0 copy-start.1
  3.2 1.0 %copy-done.1 = bf16[64,32,128]{2,1,0:T(8,128)(2,1)S(1)} copy-done((bf16[64,32,128]{2,1,0:T(8,128)(2,1)S(1)}, bf16[64,32,128]{2,1,0:T(8,128)(2,1)}, u32[]{:S(2)}) %copy-start.1) | copy-done | bytes 524312
  4.2 0.0 copy-start.2
  4.2 0.7 copy-done.2
  5.0 0.0 copy-start.3
  5.0 0.7 copy-done.3
  5.7 1.2 %pack.1 = bf16[16,34,4,128]{3,2,1,0:T(4,128)(2,1)} custom-call(s32[32,64]{1,0:T(8,128)S(1)} %bitcast.19, s32[16,64]{1,0:T(8,128)S(1)} %bitcast.20, bf16[64,8,4,128]{3,2,1,0:T(4,128)(2,1)S(1)} %bitcast.18), custom_call_target="tpu_custom_call" | custom-call | flops 1048576 | bytes 2097152 | tf_op jit(solution)/shard_map/pack/pallas_call | solution.py:141
  6.9 9.4 %all-to-all-start = ((bf16[16,34,4,128]{3,2,1,0:T(4,128)(2,1)}), bf16[16,34,4,128]{3,2,1,0:T(4,128)(2,1)S(1)}, u32[]{:S(2)}, u32[]{:S(2)}) async-start(bf16[16,34,4,128]{3,2,1,0:T(4,128)(2,1)} %pack.1), calls=%async_computation | async-start | bytes 1114112 | tf_op jit(solution)/shard_map/all_to_all | solution.py:151
  16.3 0.0 copy-done
  16.3 1.0 %fusion.2 = f32[512,512]{1,0:T(8,128)S(1)} fusion(f32[512,512]{1,0:T(8,128)S(1)} %copy-done), kind=kOutput, calls=%fused_computation.5 | convolution fusion | flops 805830656 | bytes 2097152 | tf_op jit(solution)/shard_map/dot_general | solution.py:154
  17.3 1.0 fusion.1.early_ref
  18.3 13.2 %all-to-all-done = bf16[16,34,4,128]{3,2,1,0:T(4,128)(2,1)S(1)} async-done(((bf16[16,34,4,128]{3,2,1,0:T(4,128)(2,1)}), bf16[16,34,4,128]{3,2,1,0:T(4,128)(2,1)S(1)}, u32[]{:S(2)}, u32[]{:S(2)}) %all-to-all-start) | async-done | bytes 557088 | tf_op jit(solution)/shard_map/all_to_all | solution.py:151
  31.5 0.0 collective-permute-done.other_ref
  31.5 0.0 copy-start.4
  31.5 2.2 %copy-done.4 = bf16[4096,512]{1,0:T(8,128)(2,1)S(1)} copy-done((bf16[4096,512]{1,0:T(8,128)(2,1)S(1)}, bf16[4096,512]{1,0:T(8,128)(2,1)}, u32[]{:S(2)}) %copy-start.4) | copy-done | bytes 4194328
  33.7 12.8 %project.1 = f32[512,512]{1,0:T(8,128)S(1)} custom-call(s32[1]{0:T(128)} %bitcast.core_ref, bf16[16,136,128]{2,1,0:T(8,128)(2,1)S(1)} %bitcast.17, bf16[4096,512]{1,0:T(8,128)(2,1)S(1)} %copy-done.4, bf16[4096,512]{1,0:T(8,128)(2,1)} %collective-permute-done.other_ref, f32[512,512]{1,0:T(8,128)S(1)} %fusion.1.early_ref), custom_call_target="tpu_custom_call" | custom-call | flops 4294967296 | bytes 12582912 | tf_op jit(solution)/shard_map/project/pallas_call | solution.py:158
  46.5 0.1 multiply_convert_fusion
  46.6 16.3 %all_to_all.20 = f16[16,32,512]{2,1,0:T(8,128)(2,1)S(1)} all-to-all(f16[16,32,512]{2,1,0:T(8,128)(2,1)S(1)} %bitcast.23), channel_id=1, replica_groups=mesh['zh'=2,'x'=4,'c'=2,'zl'=4,'y'=4] {'y','x'}, dimensions={0} | all-to-all | bytes 1048576 | tf_op jit(solution)/shard_map/all_to_all | solution.py:181
  62.9 0.1 convert_reduce_fusion
  63.0 16.4 %all_to_all.21 = f16[8,32,512]{2,1,0:T(8,128)(2,1)S(1)} all-to-all(f16[8,32,512]{2,1,0:T(8,128)(2,1)S(1)} %broadcast_in_dim.4), channel_id=1, replica_groups=mesh['zh'=2,'x'=4,'c'=2,'zl'=4,'y'=4] {'zh','zl'}, dimensions={0} | all-to-all | bytes 524288 | tf_op jit(solution)/shard_map/all_to_all | solution.py:184
  79.6 13.0 %all_to_all.22 = f16[16,32,512]{2,1,0:T(8,128)(2,1)S(1)} all-to-all(f16[16,32,512]{2,1,0:T(8,128)(2,1)S(1)} %broadcast_in_dim.5), channel_id=1, replica_groups=mesh['zh'=2,'x'=4,'c'=2,'zl'=4,'y'=4] {'y','x'}, dimensions={0} | all-to-all | bytes 1048576 | tf_op jit(solution)/shard_map/all_to_all | solution.py:187
  92.6 0.1 convert_multiply_fusion
  92.8 1.0 fusion
  93.8 1.0 fusion.3
  94.8 4.0 %collective-permute-start.1 = (f32[512,512]{1,0:T(8,128)S(1)}, f32[512,512]{1,0:T(8,128)S(1)}, u32[]{:S(2)}, u32[]{:S(2)}) collective-permute-start(f32[512,512]{1,0:T(8,128)S(1)} %fusion.3), channel_id=1, source_target_pairs={{0,16},{16,0},{1,17},{17,1},{2,18},{18,2},{3,19},{19,3},{4,20},{20... | collective-permute-start | bytes 3145736 | tf_op jit(solution)/shard_map/ppermute | solution.py:192
  98.8 2.3 %collective-permute-done.1 = f32[512,512]{1,0:T(8,128)S(1)} collective-permute-done((f32[512,512]{1,0:T(8,128)S(1)}, f32[512,512]{1,0:T(8,128)S(1)}, u32[]{:S(2)}, u32[]{:S(2)}) %collective-permute-start.1) | collective-permute-done | bytes 1048608 | tf_op jit(solution)/shard_map/ppermute | solution.py:192
  101.1 1.3 %multiply_subtract_fusion = f32[512,512]{1,0:T(8,128)} fusion(f32[512,512]{1,0:T(8,128)S(1)} %fusion.1.early_ref, f32[512,512]{1,0:T(8,128)S(1)} %fusion.3, f32[512,512]{1,0:T(8,128)S(1)} %collective-permute-done.1), kind=kLoop, calls=%fused_computation.6 | loop fusion | flops 786432 | bytes 4194304 | tf_op jit(solution)/shard_map/sub | solution.py:192
  (5 shorter events, 0.1 us)
Async XLA Ops:
  0.0 16.3 %copy-start = (f32[512,512]{1,0:T(8,128)S(1)}, f32[512,512]{1,0:T(8,128)}, u32[]{:S(2)}) copy-start(f32[512,512]{1,0:T(8,128)} %param.9) | copy-start | bytes 3145732
  0.0 31.5 %collective-permute-start = (bf16[4096,512]{1,0:T(8,128)(2,1)}, bf16[4096,512]{1,0:T(8,128)(2,1)}, u32[]{:S(2)}, u32[]{:S(2)}) collective-permute-start(bf16[4096,512]{1,0:T(8,128)(2,1)} %own_ref.1), channel_id=1, source_target_pairs={{0,16},{16,0},{1,17},{17,1},{2,18},{18,2},{3,19},{19,3},{4,20},{20... | collective-permute-start | bytes 12582920 | tf_op jit(solution)/shard_map/ppermute | solution.py:139
  3.2 1.0 %copy-start.1 = (bf16[64,32,128]{2,1,0:T(8,128)(2,1)S(1)}, bf16[64,32,128]{2,1,0:T(8,128)(2,1)}, u32[]{:S(2)}) copy-start(bf16[64,32,128]{2,1,0:T(8,128)(2,1)} %param.5) | copy-start | bytes 1572868
  4.2 0.7 copy-start.2
  5.0 0.7 copy-start.3
  6.9 24.6 %all-to-all-start = ((bf16[16,34,4,128]{3,2,1,0:T(4,128)(2,1)}), bf16[16,34,4,128]{3,2,1,0:T(4,128)(2,1)S(1)}, u32[]{:S(2)}, u32[]{:S(2)}) async-start(bf16[16,34,4,128]{3,2,1,0:T(4,128)(2,1)} %pack.1), calls=%async_computation | async-start | bytes 1114112 | tf_op jit(solution)/shard_map/all_to_all | solution.py:151
  31.5 2.2 %copy-start.4 = (bf16[4096,512]{1,0:T(8,128)(2,1)S(1)}, bf16[4096,512]{1,0:T(8,128)(2,1)}, u32[]{:S(2)}) copy-start(bf16[4096,512]{1,0:T(8,128)(2,1)} %own_ref.1) | copy-start | bytes 12582916
  94.8 6.3 %collective-permute-start.1 = (f32[512,512]{1,0:T(8,128)S(1)}, f32[512,512]{1,0:T(8,128)S(1)}, u32[]{:S(2)}, u32[]{:S(2)}) collective-permute-start(f32[512,512]{1,0:T(8,128)S(1)} %fusion.3), channel_id=1, source_target_pairs={{0,16},{16,0},{1,17},{17,1},{2,18},{18,2},{3,19},{19,3},{4,20},{20... | collective-permute-start | bytes 3145736 | tf_op jit(solution)/shard_map/ppermute | solution.py:192

commit v3 on v2

--- a/solution.py
+++ b/solution.py
@@ -90,28 +90,26 @@
     core = core_ref[0]
     tiles_step = depth // width
 
-    def one_step(step):
+    out_ref[...] = jnp.zeros_like(out_ref)
+
+    @pl.loop(0, 2 * STEPS)
+    def _(step):
+        pltpu.make_async_copy(own_ref.at[pl.ds(0, depth)], weights.at[step], sems.at[step]).wait()
         block = jnp.where(step < STEPS, core, 1 - core)
         base = (lax.rem(step, STEPS) * tiles_step).astype(jnp.float32)
-        base = jnp.full((1, width), base, jnp.float32).astype(jnp.bfloat16)
-        tile_a = tiles[block * 2] - base
-        tile_b = tiles[block * 2 + 1] - base
-        value_a = values[block * 2]
-        value_b = values[block * 2 + 1]
-        none = jnp.zeros_like(value_a)
-        parts = []
-        for t in range(tiles_step):
-            mark = jnp.full((1, width), t, jnp.bfloat16)
-            parts.append(jnp.where(tile_a == mark, value_a, jnp.where(tile_b == mark, value_b, none)))
-        dense = jnp.concatenate(parts, axis=1)
-        pltpu.make_async_copy(own_ref.at[pl.ds(0, depth)], weights.at[step], sems.at[step]).wait()
-        return jnp.dot(dense, weights[step], preferred_element_type=jnp.float32)
-
-    out_ref[...] = one_step(jnp.int32(0))
-
-    @pl.loop(1, 2 * STEPS)
-    def _(step):
-        out_ref[...] += one_step(step)
+        total = out_ref[...]
+        for chunk in range(tiles_step // 2):
+            parts = []
+            for t in (2 * chunk, 2 * chunk + 1):
+                mark = jnp.full((1, width), base + t, jnp.float32).astype(jnp.bfloat16)
+                parts.append(jnp.where(
+                    tiles[block * 2] == mark, values[block * 2],
+                    jnp.where(tiles[block * 2 + 1] == mark, values[block * 2 + 1], jnp.zeros((), jnp.bfloat16))))
+            dense = jnp.concatenate(parts, axis=1)
+            total = total + jnp.dot(
+                dense, weights[step, 2 * chunk * width:2 * (chunk + 1) * width, :],
+                preferred_element_type=jnp.float32)
+        out_ref[...] = total
 
 
 def to_half(values, scale):
@@ -135,6 +133,7 @@
     swap = [(0, 1), (1, 0)]
     vmem = pl.BlockSpec(memory_space=pltpu.VMEM)
     anywhere = pl.BlockSpec(memory_space=pl.ANY)
+    hbm = pl.BlockSpec(memory_space=pltpu.HBM)
 
     other = lax.ppermute(whitening, "c", swap)
     units = doc_local // 2 + 2
@@ -144,7 +143,7 @@
         in_specs=[vmem, vmem, anywhere],
         out_specs=vmem,
         scratch_shapes=[pltpu.SemaphoreType.DMA((doc_devices,))],
-        compiler_params=pltpu.CompilerParams(vmem_limit_bytes=8 << 20),
+        compiler_params=pltpu.CompilerParams(vmem_limit_bytes=61 << 20),
         cost_estimate=pl.CostEstimate(flops=1 << 20, bytes_accessed=2 << 20, transcendentals=0),
         name="pack",
     )(tile_index.T, tile_count.T, counts.reshape(doc_local, chips, group, width))
@@ -158,7 +157,7 @@
     terms = pl.pallas_call(
         project_kernel,
         out_shape=jax.ShapeDtypeStruct((half, topics), jnp.float32),
-        in_specs=[pl.BlockSpec(memory_space=pltpu.SMEM), vmem, anywhere, anywhere, anywhere],
+        in_specs=[pl.BlockSpec(memory_space=pltpu.SMEM), vmem, hbm, hbm, anywhere],
         out_specs=vmem,
         scratch_shapes=[
             pltpu.VMEM((2 * STEPS, depth, topics), jnp.bfloat16),
@@ -167,7 +166,7 @@
             pltpu.VMEM((group, half, width), jnp.bfloat16),
             pltpu.SemaphoreType.DMA((2 * STEPS,)),
         ],
-        compiler_params=pltpu.CompilerParams(vmem_limit_bytes=24 << 20),
+        compiler_params=pltpu.CompilerParams(vmem_limit_bytes=50 << 20),
         cost_estimate=pl.CostEstimate(
             flops=4 * half * whitening.shape[0] * topics, bytes_accessed=12 << 20, transcendentals=0),
         name="project",

time: 103 us -> 94.2 us (0.915)
  local copies, waits for them, and re-layouts: 4.72 us -> 0.07 us
  Pallas kernels: 14 us -> 9.97 us
    pallas_call x1, Pallas kernels: 12.8 us -> 7.29 us  [shards(): pl.pallas_call(project_kernel, out_shape=jax.ShapeDtypeStruct((half, topi...]
    unnamed x10 -> x2, local copies, waits for them, and re-layouts: 4.65 us -> 0.01 us
    pallas_call x1, Pallas kernels: 1.24 us -> 2.69 us  [shards(): pl.pallas_call(pack_kernel, out_shape=jax.ShapeDtypeStruct((doc_devices,...]
  transfers between devices with their start and end apart: 3 -> 3, of which waited for: 2 -> 2; matrix products, arithmetic and copies ran while one was open for 2% -> 2% of each run, Pallas kernels for 1% -> 3%
where the time goes in v3:
time: 94.2 us; the launch traced here: 93.8 us
  blocking collectives  45.8 us (49%)
  starting transfers between devices  16.6 us (18%)
  waiting for transfers between devices  15.5 us (16%)
  Pallas kernels  9.97 us (11%)
  matrix products  4.08 us (4%)
  other arithmetic  1.74 us (2%)
    all_to_all x2, blocking collectives, shards(): got = lax.all_to_all(sent, plane_axes, 0, 0, tiled=True)  29.3 us
    all_to_all x1, blocking collectives, shards(): got = lax.all_to_all(sent, column_axes, 0, 0, tiled=True)  16.5 us
    all_to_all x1, waiting for transfers between devices, shards(): moved = lax.all_to_all(packed, doc_axes, 0, 0, tiled=True)  13.2 us
    all_to_all x1, starting transfers between devices, shards(): moved = lax.all_to_all(packed, doc_axes, 0, 0, tiled=True)  9.36 us
    pallas_call x1, Pallas kernels, shards(): pl.pallas_call(project_kernel, out_shape=jax.ShapeDtypeStruct((half, topi...  7.29 us
    ppermute x1, starting transfers between devices, shards(): lax.ppermute(moment, 'c', swap)  4.04 us
    ppermute x1, starting transfers between devices, shards(): other = lax.ppermute(whitening, 'c', swap)  3.2 us
    pallas_call x1, Pallas kernels, shards(): pl.pallas_call(pack_kernel, out_shape=jax.ShapeDtypeStruct((doc_devices,...  2.69 us
  transfers between devices with their start and end apart: 3, of which 2 were waited for; matrix products, arithmetic and copies ran while one was open for 2% of the time, Pallas kernels for 3%

profile of v3, /device:TPU:1, one launch (start us, length us, event | category | flops | bytes accessed | tf_op | source)
XLA Modules:
  0.0 93.8 jit_solution(13593855038238190487)
XLA Ops:
  0.0 0.0 copy-start
  0.0 3.2 %collective-permute-start = (bf16[4096,512]{1,0:T(8,128)(2,1)}, bf16[4096,512]{1,0:T(8,128)(2,1)}, u32[]{:S(2)}, u32[]{:S(2)}) collective-permute-start(bf16[4096,512]{1,0:T(8,128)(2,1)} %own_ref.1), channel_id=1, source_target_pairs={{0,16},{16,0},{1,17},{17,1},{2,18},{18,2},{3,19},{19,3},{4,20},{20... | collective-permute-start | bytes 12582920 | tf_op jit(solution)/shard_map/ppermute | solution.py:138
  3.2 2.7 %pack.1 = bf16[16,34,4,128]{3,2,1,0:T(4,128)(2,1)} custom-call(s32[32,64]{1,0:T(8,128)} %bitcast.22, s32[16,64]{1,0:T(8,128)} %bitcast.23, bf16[64,8,4,128]{3,2,1,0:T(4,128)(2,1)} %bitcast.21), custom_call_target="tpu_custom_call" | custom-call | flops 1048576 | bytes 2097152 | tf_op jit(solution)/shard_map/pack/pallas_call | solution.py:140
  5.9 9.4 %all-to-all-start = ((bf16[16,34,4,128]{3,2,1,0:T(4,128)(2,1)}), bf16[16,34,4,128]{3,2,1,0:T(4,128)(2,1)S(1)}, u32[]{:S(2)}, u32[]{:S(2)}) async-start(bf16[16,34,4,128]{3,2,1,0:T(4,128)(2,1)} %pack.1), calls=%async_computation | async-start | bytes 1114112 | tf_op jit(solution)/shard_map/all_to_all | solution.py:150
  15.3 0.0 copy-done
  15.3 1.0 %fusion.2 = f32[512,512]{1,0:T(8,128)S(1)} fusion(f32[512,512]{1,0:T(8,128)S(1)} %copy-done), kind=kOutput, calls=%fused_computation.5 | convolution fusion | flops 805830656 | bytes 2097152 | tf_op jit(solution)/shard_map/dot_general | solution.py:153
  16.3 1.0 %fusion.1.early_ref = f32[512,512]{1,0:T(8,128)S(1)} fusion(f32[512,512]{1,0:T(8,128)S(1)} %fusion.2, f32[512,512]{1,0:T(8,128)S(1)} %copy-done), kind=kOutput, calls=%fused_computation.3 | convolution fusion | flops 805568512 | bytes 3145728 | tf_op jit(solution)/shard_map/dot_general | solution.py:154
  17.3 13.2 %all-to-all-done = bf16[16,34,4,128]{3,2,1,0:T(4,128)(2,1)S(1)} async-done(((bf16[16,34,4,128]{3,2,1,0:T(4,128)(2,1)}), bf16[16,34,4,128]{3,2,1,0:T(4,128)(2,1)S(1)}, u32[]{:S(2)}, u32[]{:S(2)}) %all-to-all-start) | async-done | bytes 557088 | tf_op jit(solution)/shard_map/all_to_all | solution.py:150
  30.5 0.0 collective-permute-done.other_ref
  30.5 7.3 %project.1 = f32[512,512]{1,0:T(8,128)S(1)} custom-call(s32[1]{0:T(128)} %bitcast.core_ref, bf16[16,136,128]{2,1,0:T(8,128)(2,1)S(1)} %bitcast.17, bf16[4096,512]{1,0:T(8,128)(2,1)} %own_ref.1, bf16[4096,512]{1,0:T(8,128)(2,1)} %collective-permute-done.other_ref, f32[512,512]{1,0:T(8,128)S(1)} %fusion.1.early_ref), custom_call_target="tpu_custom_call" | custom-call | flops 4294967296 | bytes 12582912 | tf_op jit(solution)/shard_map/project/pallas_call | solution.py:157
  37.8 0.1 multiply_convert_fusion
  37.9 16.3 %all_to_all.20 = f16[16,32,512]{2,1,0:T(8,128)(2,1)S(1)} all-to-all(f16[16,32,512]{2,1,0:T(8,128)(2,1)S(1)} %bitcast.20), channel_id=1, replica_groups=mesh['zh'=2,'x'=4,'c'=2,'zl'=4,'y'=4] {'y','x'}, dimensions={0} | all-to-all | bytes 1048576 | tf_op jit(solution)/shard_map/all_to_all | solution.py:180
  54.3 0.1 convert_reduce_fusion
  54.4 16.5 %all_to_all.21 = f16[8,32,512]{2,1,0:T(8,128)(2,1)S(1)} all-to-all(f16[8,32,512]{2,1,0:T(8,128)(2,1)S(1)} %broadcast_in_dim.4), channel_id=1, replica_groups=mesh['zh'=2,'x'=4,'c'=2,'zl'=4,'y'=4] {'zh','zl'}, dimensions={0} | all-to-all | bytes 524288 | tf_op jit(solution)/shard_map/all_to_all | solution.py:183
  70.9 13.0 %all_to_all.22 = f16[16,32,512]{2,1,0:T(8,128)(2,1)S(1)} all-to-all(f16[16,32,512]{2,1,0:T(8,128)(2,1)S(1)} %broadcast_in_dim.5), channel_id=1, replica_groups=mesh['zh'=2,'x'=4,'c'=2,'zl'=4,'y'=4] {'y','x'}, dimensions={0} | all-to-all | bytes 1048576 | tf_op jit(solution)/shard_map/all_to_all | solution.py:186
  83.9 0.1 convert_multiply_fusion
  84.1 1.0 %fusion = f32[512,512]{1,0:T(8,128)S(1)} fusion(f32[512,512]{1,0:T(8,128)S(1)} %bitcast.18, f32[512,512]{1,0:T(8,128)S(1)} %copy-done), kind=kOutput, calls=%fused_computation.1 | convolution fusion | flops 805830656 | bytes 3145728 | tf_op jit(solution)/shard_map/dot_general | solution.py:189
  85.1 1.0 %fusion.3 = f32[512,512]{1,0:T(8,128)S(1)} fusion(f32[512,512]{1,0:T(8,128)S(1)} %bitcast.19, f32[512,512]{1,0:T(8,128)S(1)} %fusion), kind=kOutput, calls=%fused_computation.12 | convolution fusion | flops 805306368 | bytes 3145728 | tf_op jit(solution)/shard_map/dot_general | solution.py:190
  86.1 4.0 %collective-permute-start.1 = (f32[512,512]{1,0:T(8,128)S(1)}, f32[512,512]{1,0:T(8,128)S(1)}, u32[]{:S(2)}, u32[]{:S(2)}) collective-permute-start(f32[512,512]{1,0:T(8,128)S(1)} %fusion.3), channel_id=1, source_target_pairs={{0,16},{16,0},{1,17},{17,1},{2,18},{18,2},{3,19},{19,3},{4,20},{20... | collective-permute-start | bytes 3145736 | tf_op jit(solution)/shard_map/ppermute | solution.py:191
  90.2 2.3 %collective-permute-done.1 = f32[512,512]{1,0:T(8,128)S(1)} collective-permute-done((f32[512,512]{1,0:T(8,128)S(1)}, f32[512,512]{1,0:T(8,128)S(1)}, u32[]{:S(2)}, u32[]{:S(2)}) %collective-permute-start.1) | collective-permute-done | bytes 1048608 | tf_op jit(solution)/shard_map/ppermute | solution.py:191
  92.5 1.3 %multiply_subtract_fusion = f32[512,512]{1,0:T(8,128)} fusion(f32[512,512]{1,0:T(8,128)S(1)} %fusion.1.early_ref, f32[512,512]{1,0:T(8,128)S(1)} %fusion.3, f32[512,512]{1,0:T(8,128)S(1)} %collective-permute-done.1), kind=kLoop, calls=%fused_computation.6 | loop fusion | flops 786432 | bytes 4194304 | tf_op jit(solution)/shard_map/sub | solution.py:191
  (5 shorter events, 0.1 us)
Async XLA Ops:
  0.0 15.3 %copy-start = (f32[512,512]{1,0:T(8,128)S(1)}, f32[512,512]{1,0:T(8,128)}, u32[]{:S(2)}) copy-start(f32[512,512]{1,0:T(8,128)} %param.9) | copy-start | bytes 3145732
  0.0 30.5 %collective-permute-start = (bf16[4096,512]{1,0:T(8,128)(2,1)}, bf16[4096,512]{1,0:T(8,128)(2,1)}, u32[]{:S(2)}, u32[]{:S(2)}) collective-permute-start(bf16[4096,512]{1,0:T(8,128)(2,1)} %own_ref.1), channel_id=1, source_target_pairs={{0,16},{16,0},{1,17},{17,1},{2,18},{18,2},{3,19},{19,3},{4,20},{20... | collective-permute-start | bytes 12582920 | tf_op jit(solution)/shard_map/ppermute | solution.py:138
  5.9 24.6 %all-to-all-start = ((bf16[16,34,4,128]{3,2,1,0:T(4,128)(2,1)}), bf16[16,34,4,128]{3,2,1,0:T(4,128)(2,1)S(1)}, u32[]{:S(2)}, u32[]{:S(2)}) async-start(bf16[16,34,4,128]{3,2,1,0:T(4,128)(2,1)} %pack.1), calls=%async_computation | async-start | bytes 1114112 | tf_op jit(solution)/shard_map/all_to_all | solution.py:150
  86.1 6.3 %collective-permute-start.1 = (f32[512,512]{1,0:T(8,128)S(1)}, f32[512,512]{1,0:T(8,128)S(1)}, u32[]{:S(2)}, u32[]{:S(2)}) collective-permute-start(f32[512,512]{1,0:T(8,128)S(1)} %fusion.3), channel_id=1, source_target_pairs={{0,16},{16,0},{1,17},{17,1},{2,18},{18,2},{3,19},{19,3},{4,20},{20... | collective-permute-start | bytes 3145736 | tf_op jit(solution)/shard_map/ppermute | solution.py:191

commit v4 on v3

--- a/solution.py
+++ b/solution.py
@@ -1,4 +1,3 @@
-import functools
 import math
 
 import jax
@@ -8,39 +7,48 @@
 from jax.experimental.pallas import tpu as pltpu
 from jax.sharding import Mesh, PartitionSpec as P
 
+
 penalty = 0.25
 term_scale = 256.0
 total_scale = 4.0
 HIGH = lax.Precision.HIGH
 STEPS = 4
-
-
-def pack_kernel(index_ref, live_ref, counts_ref, out_ref, sems):
-    targets, units, group, width = out_ref.shape
+PROJECT_VMEM = 50 << 20
+
+
+def pack_kernel(side_ref, index_ref, live_ref, counts_ref, near_ref, far_ref, sems):
+    targets, units, group, width = near_ref.shape
     chips = targets // 2
     docs = units - 2
+    side = side_ref[0]
     copies = []
-    for chip in range(chips):
-        for core in range(2):
-            target = chip * 2 + core
-            copy = pltpu.make_async_copy(
-                counts_ref.at[pl.ds(core * docs, docs), chip],
-                out_ref.at[target, pl.ds(0, docs)],
-                sems.at[target],
-            )
-            copy.start()
-            copies.append(copy)
+    for far, out_ref in ((1, far_ref), (0, near_ref)):
+        first = jnp.where(far == 1, 1 - side, side) * chips
+        for chip in range(chips):
+            for core in range(2):
+                target = chip * 2 + core
+                copy = pltpu.make_async_copy(
+                    counts_ref.at[pl.ds(core * docs, docs), first + chip],
+                    out_ref.at[target, pl.ds(0, docs)],
+                    sems.at[far * targets + target],
+                )
+                copy.start()
+                copies.append(copy)
     slots = group // 2
     marked = []
     for lane in range(group):
-        tile = index_ref[pl.ds(lane, chips, stride=group), :]
-        live = live_ref[pl.ds(lane // slots, chips, stride=2), :]
+        tile = index_ref[pl.ds(lane, 2 * chips, stride=group), :]
+        live = live_ref[pl.ds(lane // slots, 2 * chips, stride=2), :]
         marked.append(jnp.where(lane % slots < live, tile, -1).astype(jnp.float32))
     for core in range(2):
         rows = jnp.concatenate([m[:, core * docs:(core + 1) * docs] for m in marked], axis=1)
         for chip in range(chips):
-            row = jnp.broadcast_to(rows[chip:chip + 1, :], (2 * group, width))
-            out_ref[chip * 2 + core, docs:docs + 2] = row.reshape(2, group, width).astype(out_ref.dtype)
+            low, high = rows[chip:chip + 1, :], rows[chips + chip:chips + chip + 1, :]
+            near = jnp.where(side == 0, low, high)
+            far = jnp.where(side == 0, high, low)
+            for row, out_ref in ((near, near_ref), (far, far_ref)):
+                row = jnp.broadcast_to(row, (2 * group, width))
+                out_ref[chip * 2 + core, docs:docs + 2] = row.reshape(2, group, width).astype(out_ref.dtype)
     for copy in copies:
         copy.wait()
 
@@ -52,13 +60,11 @@
     data = rows - 2 * group
     docs = data // group
     depth = own_ref.shape[0] // STEPS
-    copies = []
     for step in range(2 * STEPS):
         source = own_ref if step < STEPS else other_ref
         copy = pltpu.make_async_copy(
             source.at[pl.ds((step % STEPS) * depth, depth)], weights.at[step], sems.at[step])
         copy.start()
-        copies.append(copy)
 
     sub = lax.broadcasted_iota(jnp.int32, (8, width), 0)
     halves = []
@@ -133,44 +139,56 @@
     swap = [(0, 1), (1, 0)]
     vmem = pl.BlockSpec(memory_space=pltpu.VMEM)
     anywhere = pl.BlockSpec(memory_space=pl.ANY)
-    hbm = pl.BlockSpec(memory_space=pltpu.HBM)
-
-    other = lax.ppermute(whitening, "c", swap)
+
+    side = lax.axis_index("zh").astype(jnp.int32)
+    core = lax.axis_index("c").astype(jnp.int32)
+    cross_axes = ("x", "c")
+    targets = lax.axis_size(cross_axes)
     units = doc_local // 2 + 2
-    packed = pl.pallas_call(
+    packed = jax.ShapeDtypeStruct((targets, units, group, width), jnp.bfloat16)
+    near, far = pl.pallas_call(
         pack_kernel,
-        out_shape=jax.ShapeDtypeStruct((doc_devices, units, group, width), jnp.bfloat16),
-        in_specs=[vmem, vmem, anywhere],
-        out_specs=vmem,
-        scratch_shapes=[pltpu.SemaphoreType.DMA((doc_devices,))],
+        out_shape=(packed, packed),
+        in_specs=[pl.BlockSpec(memory_space=pltpu.SMEM), vmem, vmem, anywhere],
+        out_specs=(vmem, vmem),
+        scratch_shapes=[pltpu.SemaphoreType.DMA((2 * targets,))],
         compiler_params=pltpu.CompilerParams(vmem_limit_bytes=61 << 20),
         cost_estimate=pl.CostEstimate(flops=1 << 20, bytes_accessed=2 << 20, transcendentals=0),
         name="pack",
-    )(tile_index.T, tile_count.T, counts.reshape(doc_local, chips, group, width))
-    moved = lax.all_to_all(packed, doc_axes, 0, 0, tiled=True)
-    moved = moved.reshape(doc_devices, units * group, width)
+    )(side.reshape(1), tile_index.T, tile_count.T, counts.reshape(doc_local, chips, group, width))
+    far = lax.ppermute(far, "zh", swap)
+    other = lax.ppermute(whitening, "c", swap)
+    near = lax.all_to_all(near, cross_axes, 0, 0, tiled=True)
+    far = lax.all_to_all(far, cross_axes, 0, 0, tiled=True)
 
     gram_matrix = jnp.dot(factors.T, factors, precision=HIGH) / topics
     early = penalty * jnp.dot(factors, gram_matrix * gram_matrix, precision=HIGH)
-    core = lax.axis_index("c")
     depth = whitening.shape[0] // STEPS
-    terms = pl.pallas_call(
-        project_kernel,
-        out_shape=jax.ShapeDtypeStruct((half, topics), jnp.float32),
-        in_specs=[pl.BlockSpec(memory_space=pltpu.SMEM), vmem, hbm, hbm, anywhere],
-        out_specs=vmem,
-        scratch_shapes=[
-            pltpu.VMEM((2 * STEPS, depth, topics), jnp.bfloat16),
-            pltpu.VMEM((half * group, width), jnp.float32),
-            pltpu.VMEM((group, half, width), jnp.bfloat16),
-            pltpu.VMEM((group, half, width), jnp.bfloat16),
-            pltpu.SemaphoreType.DMA((2 * STEPS,)),
-        ],
-        compiler_params=pltpu.CompilerParams(vmem_limit_bytes=50 << 20),
-        cost_estimate=pl.CostEstimate(
-            flops=4 * half * whitening.shape[0] * topics, bytes_accessed=12 << 20, transcendentals=0),
-        name="project",
-    )(core.astype(jnp.int32).reshape(1), moved, whitening, other, early)
+    quarter = half // 2
+
+    def project(moved, after):
+        return pl.pallas_call(
+            project_kernel,
+            out_shape=jax.ShapeDtypeStruct((quarter, topics), jnp.float32),
+            in_specs=[pl.BlockSpec(memory_space=pltpu.SMEM), vmem, anywhere, anywhere, anywhere],
+            out_specs=vmem,
+            scratch_shapes=[
+                pltpu.VMEM((2 * STEPS, depth, topics), jnp.bfloat16),
+                pltpu.VMEM((quarter * group, width), jnp.float32),
+                pltpu.VMEM((group, quarter, width), jnp.bfloat16),
+                pltpu.VMEM((group, quarter, width), jnp.bfloat16),
+                pltpu.SemaphoreType.DMA((2 * STEPS,)),
+            ],
+            compiler_params=pltpu.CompilerParams(vmem_limit_bytes=PROJECT_VMEM),
+            cost_estimate=pl.CostEstimate(
+                flops=4 * quarter * whitening.shape[0] * topics, bytes_accessed=10 << 20, transcendentals=0),
+            name="project",
+        )(core.reshape(1), moved.reshape(targets, units * group, width), whitening, other, after)
+
+    near_terms = project(near, early)
+    far_terms = project(far, near_terms)
+    terms = jnp.concatenate([
+        jnp.where(side == 0, near_terms, far_terms), jnp.where(side == 0, far_terms, near_terms)], axis=0)
 
     plane_axes, column_axes = ("y", "x"), ("zh", "zl")
     plane = lax.axis_size(plane_axes)

time: 94.2 us -> 103 us (1.093)
  waiting for transfers between devices: 15.5 us -> 8.61 us
  starting transfers between devices: 16.6 us -> 22.1 us
  blocking collectives: 45.8 us -> 50.7 us
  Pallas kernels: 9.97 us -> 12.8 us
  matrix products: 4.08 us -> 6.26 us
    all_to_all x1 -> x2, waiting for transfers between devices: 13.2 us -> 0.01 us  [the longest x1 0.01 us: shards(): near = lax.all_to_all(near, cross_axes, 0, 0, tiled=True)]
    ppermute x0 -> x1, waiting for transfers between devices: none -> 6.32 us  [shards(): far = lax.ppermute(far, 'zh', swap)]
    ppermute x0 -> x1, starting transfers between devices: none -> 6.2 us  [shards(): far = lax.ppermute(far, 'zh', swap)]
    all_to_all x1, blocking collectives: 16.5 us -> 20 us  [shards(): got = lax.all_to_all(sent, column_axes, 0, 0, tiled=True)]
    pallas_call x2 -> x3, Pallas kernels: 9.97 us -> 12.8 us  [the longest x2 10.1 us: project(): pl.pallas_call(project_kernel, out_shape=jax.ShapeDtypeStruct((quarter, t...]
    all_to_all x2, blocking collectives: 29.3 us -> 30.7 us  [shards(): got = lax.all_to_all(sent, plane_axes, 0, 0, tiled=True)]
    dot_general x1, matrix products: 1.01 us -> 2.22 us  [shards(): jnp.dot(factors, gram_matrix * gram_matrix, precision=HIGH)]
    all_to_all x1 -> x2, starting transfers between devices: 9.36 us -> 8.56 us  [the longest x1 5.14 us: shards(): far = lax.all_to_all(far, cross_axes, 0, 0, tiled=True)]
  transfers between devices with their start and end apart: 3 -> 5, of which waited for: 2 -> 2; matrix products, arithmetic and copies ran while one was open for 2% -> 4% of each run, Pallas kernels for 3% -> 8%
where the time goes in v4:
time: 103 us
  blocking collectives  50.7 us (49%)
  starting transfers between devices  22.1 us (21%)
  Pallas kernels  12.8 us (12%)
  waiting for transfers between devices  8.61 us (8%)
  matrix products  6.26 us (6%)
  other arithmetic  1.83 us (2%)
    all_to_all x2, blocking collectives, shards(): got = lax.all_to_all(sent, plane_axes, 0, 0, tiled=True)  30.7 us
    all_to_all x1, blocking collectives, shards(): got = lax.all_to_all(sent, column_axes, 0, 0, tiled=True)  20 us
    pallas_call x2, Pallas kernels, project(): pl.pallas_call(project_kernel, out_shape=jax.ShapeDtypeStruct((quarter, t...  10.1 us
    ppermute x1, waiting for transfers between devices, shards(): far = lax.ppermute(far, 'zh', swap)  6.32 us
    ppermute x1, starting transfers between devices, shards(): far = lax.ppermute(far, 'zh', swap)  6.2 us
    all_to_all x1, starting transfers between devices, shards(): far = lax.all_to_all(far, cross_axes, 0, 0, tiled=True)  5.14 us
    ppermute x1, starting transfers between devices, shards(): lax.ppermute(moment, 'c', swap)  4.14 us
    all_to_all x1, starting transfers between devices, shards(): near = lax.all_to_all(near, cross_axes, 0, 0, tiled=True)  3.42 us
  transfers between devices with their start and end apart: 5, of which 2 were waited for; matrix products, arithmetic and copies ran while one was open for 4% of the time, Pallas kernels for 8%

profile of v4, /device:TPU:1, one launch (start us, length us, event | category | flops | bytes accessed | tf_op | source)
XLA Modules:
  0.0 102.5 jit_solution(14964882715574624356)
XLA Ops:
  0.0 0.0 copy-start
  0.0 3.2 %collective-permute-start = (bf16[4096,512]{1,0:T(8,128)(2,1)}, bf16[4096,512]{1,0:T(8,128)(2,1)}, u32[]{:S(2)}, u32[]{:S(2)}) collective-permute-start(bf16[4096,512]{1,0:T(8,128)(2,1)} %own_ref.3), channel_id=1, source_target_pairs={{0,16},{16,0},{1,17},{17,1},{2,18},{18,2},{3,19},{19,3},{4,20},{20... | collective-permute-start | bytes 12582920 | tf_op jit(solution)/shard_map/ppermute | solution.py:160
  3.2 2.7 %pack.1 = (bf16[8,34,4,128]{3,2,1,0:T(4,128)(2,1)}, bf16[8,34,4,128]{3,2,1,0:T(4,128)(2,1)}) custom-call(s32[1]{0:T(128)} %bitcast.1.side_ref, s32[32,64]{1,0:T(8,128)} %bitcast.25, s32[16,64]{1,0:T(8,128)} %bitcast.26, bf16[64,8,4,128]{3,2,1,0:T(4,128)(2,1)} %bitcast.24), custom_call_target="tpu_custom_call" | custom-call | flops 1048576 | bytes 2097152 | tf_op jit(solution)/shard_map/pack/pallas_call | solution.py:149
  5.9 3.4 %all-to-all-start = ((bf16[8,34,4,128]{3,2,1,0:T(4,128)(2,1)}), bf16[8,34,4,128]{3,2,1,0:T(4,128)(2,1)S(1)}, u32[]{:S(2)}, u32[]{:S(2)}) async-start(bf16[8,34,4,128]{3,2,1,0:T(4,128)(2,1)} %get-tuple-element.7), calls=%async_computation | async-start | bytes 557056 | tf_op jit(solution)/shard_map/all_to_all | solution.py:161
  9.3 6.2 %collective-permute-start.1 = (bf16[8,34,4,128]{3,2,1,0:T(4,128)(2,1)}, bf16[8,34,4,128]{3,2,1,0:T(4,128)(2,1)}, u32[]{:S(2)}, u32[]{:S(2)}) collective-permute-start(bf16[8,34,4,128]{3,2,1,0:T(4,128)(2,1)} %get-tuple-element.8), channel_id=1, source_target_pairs={{0,128},{128,0},{1,129},{129,1},{2,130},{130,2},{3,131},{131,3},{4... | collective-permute-start | bytes 835592 | tf_op jit(solution)/shard_map/ppermute | solution.py:159
  15.5 0.0 copy-done
  15.5 2.0 %fusion.2 = f32[512,512]{1,0:T(8,128)} fusion(f32[512,512]{1,0:T(8,128)S(1)} %copy-done), kind=kOutput, calls=%fused_computation.5 | convolution fusion | flops 805830656 | bytes 2097152 | tf_op jit(solution)/shard_map/dot_general | solution.py:164
  17.5 0.0 all-to-all-done
  17.6 6.3 %collective-permute-done.1 = bf16[8,34,4,128]{3,2,1,0:T(4,128)(2,1)} collective-permute-done((bf16[8,34,4,128]{3,2,1,0:T(4,128)(2,1)}, bf16[8,34,4,128]{3,2,1,0:T(4,128)(2,1)}, u32[]{:S(2)}, u32[]{:S(2)}) %collective-permute-start.1) | collective-permute-done | bytes 278560 | tf_op jit(solution)/shard_map/ppermute | solution.py:159
  23.9 5.1 %all-to-all-start.1 = ((bf16[8,34,4,128]{3,2,1,0:T(4,128)(2,1)}), bf16[8,34,4,128]{3,2,1,0:T(4,128)(2,1)S(1)}, u32[]{:S(2)}, u32[]{:S(2)}) async-start(bf16[8,34,4,128]{3,2,1,0:T(4,128)(2,1)} %collective-permute-done.1), calls=%async_computation.1 | async-start | bytes 557056 | tf_op jit(solution)/shard_map/all_to_all | solution.py:162
  29.0 2.2 %fusion.1.early_ref = f32[512,512]{1,0:T(8,128)S(1)} fusion(f32[512,512]{1,0:T(8,128)} %fusion.2, f32[512,512]{1,0:T(8,128)S(1)} %copy-done), kind=kOutput, calls=%fused_computation.3 | convolution fusion | flops 805568512 | bytes 3145728 | tf_op jit(solution)/shard_map/dot_general | solution.py:165
  31.2 0.0 collective-permute-done.other_ref
  31.2 5.1 %project.2.early_ref = f32[256,512]{1,0:T(8,128)S(1)} custom-call(s32[1]{0:T(128)} %bitcast.core_ref, bf16[8,136,128]{2,1,0:T(8,128)(2,1)S(1)} %bitcast.19, bf16[4096,512]{1,0:T(8,128)(2,1)} %own_ref.3, bf16[4096,512]{1,0:T(8,128)(2,1)} %collective-permute-done.other_ref, f32[512,512]{1,0:T(8,128)S(1)} %fusion.1.early_ref), custom_call_target="tpu_custom_call" | custom-call | flops 2147483648 | bytes 10485760 | tf_op jit(solution)/shard_map/project/pallas_call | solution.py:170
  36.3 0.0 all-to-all-done.1
  36.3 5.1 %project.3 = f32[256,512]{1,0:T(8,128)S(1)} custom-call(s32[1]{0:T(128)} %bitcast.core_ref, bf16[8,136,128]{2,1,0:T(8,128)(2,1)S(1)} %bitcast.20, bf16[4096,512]{1,0:T(8,128)(2,1)} %own_ref.3, bf16[4096,512]{1,0:T(8,128)(2,1)} %collective-permute-done.other_ref, f32[256,512]{1,0:T(8,128)S(1)} %project.2.early_ref), custom_call_target="tpu_custom_call" | custom-call | flops 2147483648 | bytes 10485760 | tf_op jit(solution)/shard_map/project/pallas_call | solution.py:170
  41.4 0.1 broadcast_select_fusion.1
  41.5 0.1 fusion.3
  41.7 17.4 %all_to_all.25 = f16[16,32,512]{2,1,0:T(8,128)(2,1)S(1)} all-to-all(f16[16,32,512]{2,1,0:T(8,128)(2,1)S(1)} %bitcast.23), channel_id=1, replica_groups=mesh['zh'=2,'x'=4,'c'=2,'zl'=4,'y'=4] {'y','x'}, dimensions={0} | all-to-all | bytes 1048576 | tf_op jit(solution)/shard_map/all_to_all | solution.py:198
  59.0 0.1 convert_reduce_fusion
  59.2 20.0 %all_to_all.26 = f16[8,32,512]{2,1,0:T(8,128)(2,1)S(1)} all-to-all(f16[8,32,512]{2,1,0:T(8,128)(2,1)S(1)} %broadcast_in_dim.4), channel_id=1, replica_groups=mesh['zh'=2,'x'=4,'c'=2,'zl'=4,'y'=4] {'zh','zl'}, dimensions={0} | all-to-all | bytes 524288 | tf_op jit(solution)/shard_map/all_to_all | solution.py:201
  79.3 13.3 %all_to_all.27 = f16[16,32,512]{2,1,0:T(8,128)(2,1)S(1)} all-to-all(f16[16,32,512]{2,1,0:T(8,128)(2,1)S(1)} %broadcast_in_dim.5), channel_id=1, replica_groups=mesh['zh'=2,'x'=4,'c'=2,'zl'=4,'y'=4] {'y','x'}, dimensions={0} | all-to-all | bytes 1048576 | tf_op jit(solution)/shard_map/all_to_all | solution.py:204
  92.6 0.1 convert_multiply_fusion
  92.7 1.0 fusion
  93.7 1.0 fusion.4
  94.8 4.1 %collective-permute-start.2 = (f32[512,512]{1,0:T(8,128)S(1)}, f32[512,512]{1,0:T(8,128)S(1)}, u32[]{:S(2)}, u32[]{:S(2)}) collective-permute-start(f32[512,512]{1,0:T(8,128)S(1)} %fusion.4), channel_id=1, source_target_pairs={{0,16},{16,0},{1,17},{17,1},{2,18},{18,2},{3,19},{19,3},{4,20},{20... | collective-permute-start | bytes 3145736 | tf_op jit(solution)/shard_map/ppermute | solution.py:209
  98.9 2.3 %collective-permute-done.2 = f32[512,512]{1,0:T(8,128)S(1)} collective-permute-done((f32[512,512]{1,0:T(8,128)S(1)}, f32[512,512]{1,0:T(8,128)S(1)}, u32[]{:S(2)}, u32[]{:S(2)}) %collective-permute-start.2) | collective-permute-done | bytes 1048608 | tf_op jit(solution)/shard_map/ppermute | solution.py:209
  101.2 1.3 %multiply_subtract_fusion = f32[512,512]{1,0:T(8,128)} fusion(f32[512,512]{1,0:T(8,128)S(1)} %fusion.1.early_ref, f32[512,512]{1,0:T(8,128)S(1)} %fusion.4, f32[512,512]{1,0:T(8,128)S(1)} %collective-permute-done.2), kind=kLoop, calls=%fused_computation.8 | loop fusion | flops 786432 | bytes 4194304 | tf_op jit(solution)/shard_map/sub | solution.py:209
  (5 shorter events, 0.1 us)
Async XLA Ops:
  0.0 15.5 %copy-start = (f32[512,512]{1,0:T(8,128)S(1)}, f32[512,512]{1,0:T(8,128)}, u32[]{:S(2)}) copy-start(f32[512,512]{1,0:T(8,128)} %param.9) | copy-start | bytes 3145732
  0.0 31.2 %collective-permute-start = (bf16[4096,512]{1,0:T(8,128)(2,1)}, bf16[4096,512]{1,0:T(8,128)(2,1)}, u32[]{:S(2)}, u32[]{:S(2)}) collective-permute-start(bf16[4096,512]{1,0:T(8,128)(2,1)} %own_ref.3), channel_id=1, source_target_pairs={{0,16},{16,0},{1,17},{17,1},{2,18},{18,2},{3,19},{19,3},{4,20},{20... | collective-permute-start | bytes 12582920 | tf_op jit(solution)/shard_map/ppermute | solution.py:160
  5.9 11.6 %all-to-all-start = ((bf16[8,34,4,128]{3,2,1,0:T(4,128)(2,1)}), bf16[8,34,4,128]{3,2,1,0:T(4,128)(2,1)S(1)}, u32[]{:S(2)}, u32[]{:S(2)}) async-start(bf16[8,34,4,128]{3,2,1,0:T(4,128)(2,1)} %get-tuple-element.7), calls=%async_computation | async-start | bytes 557056 | tf_op jit(solution)/shard_map/all_to_all | solution.py:161
  9.3 14.5 %collective-permute-start.1 = (bf16[8,34,4,128]{3,2,1,0:T(4,128)(2,1)}, bf16[8,34,4,128]{3,2,1,0:T(4,128)(2,1)}, u32[]{:S(2)}, u32[]{:S(2)}) collective-permute-start(bf16[8,34,4,128]{3,2,1,0:T(4,128)(2,1)} %get-tuple-element.8), channel_id=1, source_target_pairs={{0,128},{128,0},{1,129},{129,1},{2,130},{130,2},{3,131},{131,3},{4... | collective-permute-start | bytes 835592 | tf_op jit(solution)/shard_map/ppermute | solution.py:159
  23.9 12.5 %all-to-all-start.1 = ((bf16[8,34,4,128]{3,2,1,0:T(4,128)(2,1)}), bf16[8,34,4,128]{3,2,1,0:T(4,128)(2,1)S(1)}, u32[]{:S(2)}, u32[]{:S(2)}) async-start(bf16[8,34,4,128]{3,2,1,0:T(4,128)(2,1)} %collective-permute-done.1), calls=%async_computation.1 | async-start | bytes 557056 | tf_op jit(solution)/shard_map/all_to_all | solution.py:162
  94.8 6.4 %collective-permute-start.2 = (f32[512,512]{1,0:T(8,128)S(1)}, f32[512,512]{1,0:T(8,128)S(1)}, u32[]{:S(2)}, u32[]{:S(2)}) collective-permute-start(f32[512,512]{1,0:T(8,128)S(1)} %fusion.4), channel_id=1, source_target_pairs={{0,16},{16,0},{1,17},{17,1},{2,18},{18,2},{3,19},{19,3},{4,20},{20... | collective-permute-start | bytes 3145736 | tf_op jit(solution)/shard_map/ppermute | solution.py:209

commit v5 on v4

--- a/solution.py
+++ b/solution.py
@@ -159,7 +159,6 @@
     far = lax.ppermute(far, "zh", swap)
     other = lax.ppermute(whitening, "c", swap)
     near = lax.all_to_all(near, cross_axes, 0, 0, tiled=True)
-    far = lax.all_to_all(far, cross_axes, 0, 0, tiled=True)
 
     gram_matrix = jnp.dot(factors.T, factors, precision=HIGH) / topics
     early = penalty * jnp.dot(factors, gram_matrix * gram_matrix, precision=HIGH)
@@ -186,20 +185,23 @@
         )(core.reshape(1), moved.reshape(targets, units * group, width), whitening, other, after)
 
     near_terms = project(near, early)
+    far, near_terms = lax.optimization_barrier((far, near_terms))
+    far = lax.all_to_all(far, cross_axes, 0, 0, tiled=True)
     far_terms = project(far, near_terms)
     terms = jnp.concatenate([
         jnp.where(side == 0, near_terms, far_terms), jnp.where(side == 0, far_terms, near_terms)], axis=0)
 
-    plane_axes, column_axes = ("y", "x"), ("zh", "zl")
+    plane_axes = ("y", "x")
     plane = lax.axis_size(plane_axes)
-    column = lax.axis_size(column_axes)
+    column = lax.axis_size("zl")
     part = half // plane
     sent = to_half(terms, term_scale).reshape(plane, part, topics)
     got = lax.all_to_all(sent, plane_axes, 0, 0, tiled=True)
     plane_sum = jnp.sum(got.astype(jnp.float32), axis=0) * (1.0 / term_scale)
     sent = jnp.broadcast_to(to_half(plane_sum, total_scale)[None], (column, part, topics))
-    got = lax.all_to_all(sent, column_axes, 0, 0, tiled=True)
+    got = lax.all_to_all(sent, "zl", 0, 0, tiled=True)
     total = jnp.sum(got.astype(jnp.float32), axis=0) * (1.0 / total_scale)
+    total = total + lax.ppermute(total, "zh", swap)
     sent = jnp.broadcast_to(to_half(total, total_scale)[None], (plane, part, topics))
     got = lax.all_to_all(sent, plane_axes, 0, 0, tiled=True)
     projected = from_half(got.reshape(half, topics), total_scale)

time: 103 us -> 100 us (0.971)
  blocking collectives: 50.7 us -> 39.3 us
  starting transfers between devices: 22.1 us -> 28.9 us
  waiting for transfers between devices: 8.61 us -> 12.3 us
  matrix products: 6.26 us -> 4.08 us
    all_to_all x1, blocking collectives: 20 us -> 12.3 us  [shards(): got = lax.all_to_all(sent, 'zl', 0, 0, tiled=True)]
    all_to_all x1, waiting for transfers between devices: 0.01 us -> 6.62 us  [shards(): far = lax.all_to_all(far, cross_axes, 0, 0, tiled=True)]
    ppermute x1, waiting for transfers between devices: 6.32 us -> 1.17 us  [shards(): far = lax.ppermute(far, 'zh', swap)]
    ppermute x0 -> x1, starting transfers between devices: none -> 4.92 us  [shards(): total = total + lax.ppermute(total, 'zh', swap)]
    all_to_all x2, blocking collectives: 30.7 us -> 27 us  [shards(): got = lax.all_to_all(sent, plane_axes, 0, 0, tiled=True)]
    ppermute x0 -> x1, waiting for transfers between devices: none -> 2.19 us  [shards(): total = total + lax.ppermute(total, 'zh', swap)]
    ppermute x1, starting transfers between devices: 4.14 us -> 6.02 us  [shards(): lax.ppermute(moment, 'c', swap)]
    dot_general x1, matrix products: 2.22 us -> 1.01 us  [shards(): jnp.dot(factors, gram_matrix * gram_matrix, precision=HIGH)]
  transfers between devices with their start and end apart: 5 -> 6, of which waited for: 2 -> 4; matrix products, arithmetic and copies ran while one was open for 4% -> 2% of each run, Pallas kernels for 8% -> 8%
where the time goes in v5:
time: 100 us; the launch traced here: 99.5 us
  blocking collectives  39.3 us (39%)
  starting transfers between devices  28.9 us (29%)
  Pallas kernels  12.8 us (13%)
  waiting for transfers between devices  12.3 us (12%)
  matrix products  4.08 us (4%)
  other arithmetic  1.83 us (2%)
    all_to_all x2, blocking collectives, shards(): got = lax.all_to_all(sent, plane_axes, 0, 0, tiled=True)  27 us
    all_to_all x1, blocking collectives, shards(): got = lax.all_to_all(sent, 'zl', 0, 0, tiled=True)  12.3 us
    pallas_call x2, Pallas kernels, project(): pl.pallas_call(project_kernel, out_shape=jax.ShapeDtypeStruct((quarter, t...  10.1 us
    all_to_all x1, waiting for transfers between devices, shards(): far = lax.all_to_all(far, cross_axes, 0, 0, tiled=True)  6.62 us
    ppermute x1, starting transfers between devices, shards(): far = lax.ppermute(far, 'zh', swap)  6.2 us
    ppermute x1, starting transfers between devices, shards(): lax.ppermute(moment, 'c', swap)  6.02 us
    all_to_all x1, starting transfers between devices, shards(): far = lax.all_to_all(far, cross_axes, 0, 0, tiled=True)  5.14 us
    ppermute x1, starting transfers between devices, shards(): total = total + lax.ppermute(total, 'zh', swap)  4.92 us
  transfers between devices with their start and end apart: 6, of which 4 were waited for; matrix products, arithmetic and copies ran while one was open for 2% of the time, Pallas kernels for 8%

profile of v5, /device:TPU:1, one launch (start us, length us, event | category | flops | bytes accessed | tf_op | source)
XLA Modules:
  0.0 99.5 jit_solution(2015061960837218777)
XLA Ops:
  0.0 0.0 copy-start
  0.0 3.2 %collective-permute-start.1 = (bf16[4096,512]{1,0:T(8,128)(2,1)}, bf16[4096,512]{1,0:T(8,128)(2,1)}, u32[]{:S(2)}, u32[]{:S(2)}) collective-permute-start(bf16[4096,512]{1,0:T(8,128)(2,1)} %own_ref.3), channel_id=1, source_target_pairs={{0,16},{16,0},{1,17},{17,1},{2,18},{18,2},{3,19},{19,3},{4,20},{20... | collective-permute-start | bytes 12582920 | tf_op jit(solution)/shard_map/ppermute | solution.py:160
  3.2 2.7 %pack.1 = (bf16[8,34,4,128]{3,2,1,0:T(4,128)(2,1)}, bf16[8,34,4,128]{3,2,1,0:T(4,128)(2,1)}) custom-call(s32[1]{0:T(128)} %bitcast.side_ref, s32[32,64]{1,0:T(8,128)} %bitcast.25, s32[16,64]{1,0:T(8,128)} %bitcast.26, bf16[64,8,4,128]{3,2,1,0:T(4,128)(2,1)} %bitcast.24), custom_call_target="tpu_custom_call" | custom-call | flops 1048576 | bytes 2097152 | tf_op jit(solution)/shard_map/pack/pallas_call | solution.py:149
  5.9 3.4 %all-to-all-start = ((bf16[8,34,4,128]{3,2,1,0:T(4,128)(2,1)}), bf16[8,34,4,128]{3,2,1,0:T(4,128)(2,1)S(1)}, u32[]{:S(2)}, u32[]{:S(2)}) async-start(bf16[8,34,4,128]{3,2,1,0:T(4,128)(2,1)} %get-tuple-element.10), calls=%async_computation | async-start | bytes 557056 | tf_op jit(solution)/shard_map/all_to_all | solution.py:161
  9.3 6.2 %collective-permute-start = (bf16[8,34,4,128]{3,2,1,0:T(4,128)(2,1)}, bf16[8,34,4,128]{3,2,1,0:T(4,128)(2,1)}, u32[]{:S(2)}, u32[]{:S(2)}) collective-permute-start(bf16[8,34,4,128]{3,2,1,0:T(4,128)(2,1)} %get-tuple-element.9), channel_id=1, source_target_pairs={{0,128},{128,0},{1,129},{129,1},{2,130},{130,2},{3,131},{131,3},{4... | collective-permute-start | bytes 835592 | tf_op jit(solution)/shard_map/ppermute | solution.py:159
  15.5 0.0 copy-done
  15.5 1.0 %fusion.2 = f32[512,512]{1,0:T(8,128)S(1)} fusion(f32[512,512]{1,0:T(8,128)S(1)} %copy-done), kind=kOutput, calls=%fused_computation.5 | convolution fusion | flops 805830656 | bytes 2097152 | tf_op jit(solution)/shard_map/dot_general | solution.py:163
  16.6 1.0 %fusion.1.early_ref = f32[512,512]{1,0:T(8,128)S(1)} fusion(f32[512,512]{1,0:T(8,128)S(1)} %fusion.2, f32[512,512]{1,0:T(8,128)S(1)} %copy-done), kind=kOutput, calls=%fused_computation.3 | convolution fusion | flops 805568512 | bytes 3145728 | tf_op jit(solution)/shard_map/dot_general | solution.py:164
  17.6 0.0 all-to-all-done
  17.6 0.0 collective-permute-done.1.other_ref
  17.6 5.1 %project.2.early_ref = f32[256,512]{1,0:T(8,128)S(1)} custom-call(s32[1]{0:T(128)} %bitcast.4.core_ref, bf16[8,136,128]{2,1,0:T(8,128)(2,1)S(1)} %bitcast.19, bf16[4096,512]{1,0:T(8,128)(2,1)} %own_ref.3, bf16[4096,512]{1,0:T(8,128)(2,1)} %collective-permute-done.1.other_ref, f32[512,512]{1,0:T(8,128)S(1)} %fusion.1.early_ref), custom_call_target="tpu_custom_call" | custom-call | flops 2147483648 | bytes 10485760 | tf_op jit(solution)/shard_map/project/pallas_call | solution.py:169
  22.7 1.2 %collective-permute-done = bf16[8,34,4,128]{3,2,1,0:T(4,128)(2,1)} collective-permute-done((bf16[8,34,4,128]{3,2,1,0:T(4,128)(2,1)}, bf16[8,34,4,128]{3,2,1,0:T(4,128)(2,1)}, u32[]{:S(2)}, u32[]{:S(2)}) %collective-permute-start) | collective-permute-done | bytes 278560 | tf_op jit(solution)/shard_map/ppermute | solution.py:159
  23.9 5.1 %all-to-all-start.1 = ((bf16[8,34,4,128]{3,2,1,0:T(4,128)(2,1)}), bf16[8,34,4,128]{3,2,1,0:T(4,128)(2,1)S(1)}, u32[]{:S(2)}, u32[]{:S(2)}) async-start(bf16[8,34,4,128]{3,2,1,0:T(4,128)(2,1)} %collective-permute-done), calls=%async_computation.1 | async-start | bytes 557056 | tf_op jit(solution)/shard_map/all_to_all | solution.py:189
  29.0 6.6 %all-to-all-done.1 = bf16[8,34,4,128]{3,2,1,0:T(4,128)(2,1)S(1)} async-done(((bf16[8,34,4,128]{3,2,1,0:T(4,128)(2,1)}), bf16[8,34,4,128]{3,2,1,0:T(4,128)(2,1)S(1)}, u32[]{:S(2)}, u32[]{:S(2)}) %all-to-all-start.1) | async-done | bytes 278560 | tf_op jit(solution)/shard_map/all_to_all | solution.py:189
  35.6 5.1 %project.3 = f32[256,512]{1,0:T(8,128)S(1)} custom-call(s32[1]{0:T(128)} %bitcast.4.core_ref, bf16[8,136,128]{2,1,0:T(8,128)(2,1)S(1)} %bitcast.20, bf16[4096,512]{1,0:T(8,128)(2,1)} %own_ref.3, bf16[4096,512]{1,0:T(8,128)(2,1)} %collective-permute-done.1.other_ref, f32[256,512]{1,0:T(8,128)S(1)} %project.2.early_ref), custom_call_target="tpu_custom_call" | custom-call | flops 2147483648 | bytes 10485760 | tf_op jit(solution)/shard_map/project/pallas_call | solution.py:169
  40.7 0.1 broadcast_select_fusion.1
  40.8 0.1 fusion.3
  40.9 15.0 %all_to_all.25 = f16[16,32,512]{2,1,0:T(8,128)(2,1)S(1)} all-to-all(f16[16,32,512]{2,1,0:T(8,128)(2,1)S(1)} %bitcast.23), channel_id=1, replica_groups=mesh['zh'=2,'x'=4,'c'=2,'zl'=4,'y'=4] {'y','x'}, dimensions={0} | all-to-all | bytes 1048576 | tf_op jit(solution)/shard_map/all_to_all | solution.py:199
  56.0 0.1 convert_reduce_fusion
  56.1 12.3 %all_to_all.26 = f16[4,32,512]{2,1,0:T(8,128)(2,1)S(1)} all-to-all(f16[4,32,512]{2,1,0:T(8,128)(2,1)S(1)} %broadcast_in_dim.4), channel_id=1, replica_groups=mesh['zh'=2,'x'=4,'c'=2,'zl'=4,'y'=4] {'zl'}, dimensions={0} | all-to-all | bytes 262144 | tf_op jit(solution)/shard_map/all_to_all | solution.py:202
  68.5 4.9 %collective-permute-start.2 = (f32[32,512]{1,0:T(8,128)S(1)}, f32[32,512]{1,0:T(8,128)S(1)}, u32[]{:S(2)}, u32[]{:S(2)}) collective-permute-start(f32[32,512]{1,0:T(8,128)S(1)} %broadcast_multiply_fusion), channel_id=1, source_target_pairs={{0,128},{128,0},{1,129},{129,1},{2,130},{130,2},{3,131},{131,3},{4... | collective-permute-start | bytes 196616 | tf_op jit(solution)/shard_map/ppermute | solution.py:204
  73.4 2.2 %collective-permute-done.2 = f32[32,512]{1,0:T(8,128)S(1)} collective-permute-done((f32[32,512]{1,0:T(8,128)S(1)}, f32[32,512]{1,0:T(8,128)S(1)}, u32[]{:S(2)}, u32[]{:S(2)}) %collective-permute-start.2) | collective-permute-done | bytes 65568 | tf_op jit(solution)/shard_map/ppermute | solution.py:204
  75.6 12.0 %all_to_all.27 = f16[16,32,512]{2,1,0:T(8,128)(2,1)S(1)} all-to-all(f16[16,32,512]{2,1,0:T(8,128)(2,1)S(1)} %broadcast_in_dim.5), channel_id=1, replica_groups=mesh['zh'=2,'x'=4,'c'=2,'zl'=4,'y'=4] {'y','x'}, dimensions={0} | all-to-all | bytes 1048576 | tf_op jit(solution)/shard_map/all_to_all | solution.py:206
  87.6 0.1 convert_multiply_fusion
  87.8 1.0 %fusion = f32[512,512]{1,0:T(8,128)S(1)} fusion(f32[512,512]{1,0:T(8,128)S(1)} %bitcast.21, f32[512,512]{1,0:T(8,128)S(1)} %copy-done), kind=kOutput, calls=%fused_computation.1 | convolution fusion | flops 805830656 | bytes 3145728 | tf_op jit(solution)/shard_map/dot_general | solution.py:209
  88.8 1.0 %fusion.4 = f32[512,512]{1,0:T(8,128)S(1)} fusion(f32[512,512]{1,0:T(8,128)S(1)} %bitcast.22, f32[512,512]{1,0:T(8,128)S(1)} %fusion), kind=kOutput, calls=%fused_computation.17 | convolution fusion | flops 805306368 | bytes 3145728 | tf_op jit(solution)/shard_map/dot_general | solution.py:210
  89.8 6.0 %collective-permute-start.3 = (f32[512,512]{1,0:T(8,128)S(1)}, f32[512,512]{1,0:T(8,128)S(1)}, u32[]{:S(2)}, u32[]{:S(2)}) collective-permute-start(f32[512,512]{1,0:T(8,128)S(1)} %fusion.4), channel_id=1, source_target_pairs={{0,16},{16,0},{1,17},{17,1},{2,18},{18,2},{3,19},{19,3},{4,20},{20... | collective-permute-start | bytes 3145736 | tf_op jit(solution)/shard_map/ppermute | solution.py:211
  95.8 2.3 %collective-permute-done.3 = f32[512,512]{1,0:T(8,128)S(1)} collective-permute-done((f32[512,512]{1,0:T(8,128)S(1)}, f32[512,512]{1,0:T(8,128)S(1)}, u32[]{:S(2)}, u32[]{:S(2)}) %collective-permute-start.3) | collective-permute-done | bytes 1048608 | tf_op jit(solution)/shard_map/ppermute | solution.py:211
  98.1 1.3 %multiply_subtract_fusion = f32[512,512]{1,0:T(8,128)} fusion(f32[512,512]{1,0:T(8,128)S(1)} %fusion.1.early_ref, f32[512,512]{1,0:T(8,128)S(1)} %fusion.4, f32[512,512]{1,0:T(8,128)S(1)} %collective-permute-done.3), kind=kLoop, calls=%fused_computation.8 | loop fusion | flops 786432 | bytes 4194304 | tf_op jit(solution)/shard_map/sub | solution.py:211
  (6 shorter events, 0.1 us)
Async XLA Ops:
  0.0 15.5 %copy-start = (f32[512,512]{1,0:T(8,128)S(1)}, f32[512,512]{1,0:T(8,128)}, u32[]{:S(2)}) copy-start(f32[512,512]{1,0:T(8,128)} %param.9) | copy-start | bytes 3145732
  0.0 17.6 %collective-permute-start.1 = (bf16[4096,512]{1,0:T(8,128)(2,1)}, bf16[4096,512]{1,0:T(8,128)(2,1)}, u32[]{:S(2)}, u32[]{:S(2)}) collective-permute-start(bf16[4096,512]{1,0:T(8,128)(2,1)} %own_ref.3), channel_id=1, source_target_pairs={{0,16},{16,0},{1,17},{17,1},{2,18},{18,2},{3,19},{19,3},{4,20},{20... | collective-permute-start | bytes 12582920 | tf_op jit(solution)/shard_map/ppermute | solution.py:160
  5.9 11.7 %all-to-all-start = ((bf16[8,34,4,128]{3,2,1,0:T(4,128)(2,1)}), bf16[8,34,4,128]{3,2,1,0:T(4,128)(2,1)S(1)}, u32[]{:S(2)}, u32[]{:S(2)}) async-start(bf16[8,34,4,128]{3,2,1,0:T(4,128)(2,1)} %get-tuple-element.10), calls=%async_computation | async-start | bytes 557056 | tf_op jit(solution)/shard_map/all_to_all | solution.py:161
  9.3 14.5 %collective-permute-start = (bf16[8,34,4,128]{3,2,1,0:T(4,128)(2,1)}, bf16[8,34,4,128]{3,2,1,0:T(4,128)(2,1)}, u32[]{:S(2)}, u32[]{:S(2)}) collective-permute-start(bf16[8,34,4,128]{3,2,1,0:T(4,128)(2,1)} %get-tuple-element.9), channel_id=1, source_target_pairs={{0,128},{128,0},{1,129},{129,1},{2,130},{130,2},{3,131},{131,3},{4... | collective-permute-start | bytes 835592 | tf_op jit(solution)/shard_map/ppermute | solution.py:159
  23.9 11.8 %all-to-all-start.1 = ((bf16[8,34,4,128]{3,2,1,0:T(4,128)(2,1)}), bf16[8,34,4,128]{3,2,1,0:T(4,128)(2,1)S(1)}, u32[]{:S(2)}, u32[]{:S(2)}) async-start(bf16[8,34,4,128]{3,2,1,0:T(4,128)(2,1)} %collective-permute-done), calls=%async_computation.1 | async-start | bytes 557056 | tf_op jit(solution)/shard_map/all_to_all | solution.py:189
  68.5 7.1 %collective-permute-start.2 = (f32[32,512]{1,0:T(8,128)S(1)}, f32[32,512]{1,0:T(8,128)S(1)}, u32[]{:S(2)}, u32[]{:S(2)}) collective-permute-start(f32[32,512]{1,0:T(8,128)S(1)} %broadcast_multiply_fusion), channel_id=1, source_target_pairs={{0,128},{128,0},{1,129},{129,1},{2,130},{130,2},{3,131},{131,3},{4... | collective-permute-start | bytes 196616 | tf_op jit(solution)/shard_map/ppermute | solution.py:204
  89.8 8.3 %collective-permute-start.3 = (f32[512,512]{1,0:T(8,128)S(1)}, f32[512,512]{1,0:T(8,128)S(1)}, u32[]{:S(2)}, u32[]{:S(2)}) collective-permute-start(f32[512,512]{1,0:T(8,128)S(1)} %fusion.4), channel_id=1, source_target_pairs={{0,16},{16,0},{1,17},{17,1},{2,18},{18,2},{3,19},{19,3},{4,20},{20... | collective-permute-start | bytes 3145736 | tf_op jit(solution)/shard_map/ppermute | solution.py:211

commit v6 on v3

--- a/solution.py
+++ b/solution.py
@@ -1,4 +1,3 @@
-import functools
 import math
 
 import jax
@@ -13,23 +12,28 @@
 total_scale = 4.0
 HIGH = lax.Precision.HIGH
 STEPS = 4
-
-
-def pack_kernel(index_ref, live_ref, counts_ref, out_ref, sems):
-    targets, units, group, width = out_ref.shape
+AHEAD = 2
+
+
+def pack_kernel(index_hbm, live_hbm, counts_ref, out_ref, index_ref, live_ref, packed, small_sems, in_sems, out_sems):
+    targets, units, group, width = packed.shape
     chips = targets // 2
     docs = units - 2
+    small = [
+        pltpu.make_async_copy(index_hbm, index_ref, small_sems.at[0]),
+        pltpu.make_async_copy(live_hbm, live_ref, small_sems.at[1]),
+    ]
+    for copy in small:
+        copy.start()
     copies = []
-    for chip in range(chips):
-        for core in range(2):
-            target = chip * 2 + core
-            copy = pltpu.make_async_copy(
-                counts_ref.at[pl.ds(core * docs, docs), chip],
-                out_ref.at[target, pl.ds(0, docs)],
-                sems.at[target],
-            )
-            copy.start()
-            copies.append(copy)
+    for target in range(targets):
+        chip, core = target // 2, target % 2
+        copy = pltpu.make_async_copy(
+            counts_ref.at[pl.ds(core * docs, docs), chip], packed.at[target, pl.ds(0, docs)], in_sems.at[target])
+        copy.start()
+        copies.append(copy)
+    for copy in small:
+        copy.wait()
     slots = group // 2
     marked = []
     for lane in range(group):
@@ -40,8 +44,14 @@
         rows = jnp.concatenate([m[:, core * docs:(core + 1) * docs] for m in marked], axis=1)
         for chip in range(chips):
             row = jnp.broadcast_to(rows[chip:chip + 1, :], (2 * group, width))
-            out_ref[chip * 2 + core, docs:docs + 2] = row.reshape(2, group, width).astype(out_ref.dtype)
-    for copy in copies:
+            packed[chip * 2 + core, docs:docs + 2] = row.reshape(2, group, width).astype(packed.dtype)
+    sends = []
+    for target in range(targets):
+        copies[target].wait()
+        copy = pltpu.make_async_copy(packed.at[target], out_ref.at[target], out_sems.at[target])
+        copy.start()
+        sends.append(copy)
+    for copy in sends:
         copy.wait()
 
 
@@ -52,13 +62,13 @@
     data = rows - 2 * group
     docs = data // group
     depth = own_ref.shape[0] // STEPS
-    copies = []
-    for step in range(2 * STEPS):
-        source = own_ref if step < STEPS else other_ref
-        copy = pltpu.make_async_copy(
-            source.at[pl.ds((step % STEPS) * depth, depth)], weights.at[step], sems.at[step])
-        copy.start()
-        copies.append(copy)
+
+    def fetch(source, step):
+        pltpu.make_async_copy(
+            source.at[pl.ds(lax.rem(step, STEPS) * depth, depth)], weights.at[step], sems.at[step]).start()
+
+    for step in range(AHEAD):
+        fetch(own_ref, jnp.int32(step))
 
     sub = lax.broadcasted_iota(jnp.int32, (8, width), 0)
     halves = []
@@ -95,6 +105,15 @@
     @pl.loop(0, 2 * STEPS)
     def _(step):
         pltpu.make_async_copy(own_ref.at[pl.ds(0, depth)], weights.at[step], sems.at[step]).wait()
+
+        @pl.when(step + AHEAD < STEPS)
+        def _():
+            fetch(own_ref, step + AHEAD)
+
+        @pl.when(jnp.logical_and(step + AHEAD >= STEPS, step + AHEAD < 2 * STEPS))
+        def _():
+            fetch(other_ref, step + AHEAD)
+
         block = jnp.where(step < STEPS, core, 1 - core)
         base = (lax.rem(step, STEPS) * tiles_step).astype(jnp.float32)
         total = out_ref[...]
@@ -133,16 +152,22 @@
     swap = [(0, 1), (1, 0)]
     vmem = pl.BlockSpec(memory_space=pltpu.VMEM)
     anywhere = pl.BlockSpec(memory_space=pl.ANY)
-    hbm = pl.BlockSpec(memory_space=pltpu.HBM)
 
     other = lax.ppermute(whitening, "c", swap)
     units = doc_local // 2 + 2
     packed = pl.pallas_call(
         pack_kernel,
         out_shape=jax.ShapeDtypeStruct((doc_devices, units, group, width), jnp.bfloat16),
-        in_specs=[vmem, vmem, anywhere],
-        out_specs=vmem,
-        scratch_shapes=[pltpu.SemaphoreType.DMA((doc_devices,))],
+        in_specs=[anywhere, anywhere, anywhere],
+        out_specs=anywhere,
+        scratch_shapes=[
+            pltpu.VMEM(tile_index.shape[::-1], tile_index.dtype),
+            pltpu.VMEM(tile_count.shape[::-1], tile_count.dtype),
+            pltpu.VMEM((doc_devices, units, group, width), jnp.bfloat16),
+            pltpu.SemaphoreType.DMA((2,)),
+            pltpu.SemaphoreType.DMA((doc_devices,)),
+            pltpu.SemaphoreType.DMA((doc_devices,)),
+        ],
         compiler_params=pltpu.CompilerParams(vmem_limit_bytes=61 << 20),
         cost_estimate=pl.CostEstimate(flops=1 << 20, bytes_accessed=2 << 20, transcendentals=0),
         name="pack",
@@ -157,7 +182,7 @@
     terms = pl.pallas_call(
         project_kernel,
         out_shape=jax.ShapeDtypeStruct((half, topics), jnp.float32),
-        in_specs=[pl.BlockSpec(memory_space=pltpu.SMEM), vmem, hbm, hbm, anywhere],
+        in_specs=[pl.BlockSpec(memory_space=pltpu.SMEM), vmem, anywhere, anywhere, anywhere],
         out_specs=vmem,
         scratch_shapes=[
             pltpu.VMEM((2 * STEPS, depth, topics), jnp.bfloat16),

time: 94.2 us -> 93.6 us (level)
  transfers between devices with their start and end apart: 3 -> 3, of which waited for: 2 -> 2; matrix products, arithmetic and copies ran while one was open for 2% -> 2% of each run, Pallas kernels for 3% -> 2%
where the time goes in v6:
time: 93.6 us; the launch traced here: 93.3 us
  blocking collectives  45.8 us (49%)
  starting transfers between devices  16.6 us (18%)
  waiting for transfers between devices  15.5 us (17%)
  Pallas kernels  9.44 us (10%)
  matrix products  4.08 us (4%)
  other arithmetic  1.74 us (2%)
    all_to_all x2, blocking collectives, shards(): got = lax.all_to_all(sent, plane_axes, 0, 0, tiled=True)  29.3 us
    all_to_all x1, blocking collectives, shards(): got = lax.all_to_all(sent, column_axes, 0, 0, tiled=True)  16.5 us
    all_to_all x1, waiting for transfers between devices, shards(): moved = lax.all_to_all(packed, doc_axes, 0, 0, tiled=True)  13.2 us
    all_to_all x1, starting transfers between devices, shards(): moved = lax.all_to_all(packed, doc_axes, 0, 0, tiled=True)  9.36 us
    pallas_call x1, Pallas kernels, shards(): pl.pallas_call(project_kernel, out_shape=jax.ShapeDtypeStruct((half, topi...  7.31 us
    ppermute x1, starting transfers between devices, shards(): lax.ppermute(moment, 'c', swap)  4.01 us
    ppermute x1, starting transfers between devices, shards(): other = lax.ppermute(whitening, 'c', swap)  3.2 us
    ppermute x1, waiting for transfers between devices, shards(): lax.ppermute(moment, 'c', swap)  2.29 us
  transfers between devices with their start and end apart: 3, of which 2 were waited for; matrix products, arithmetic and copies ran while one was open for 2% of the time, Pallas kernels for 2%

profile of v6, /device:TPU:1, one launch (start us, length us, event | category | flops | bytes accessed | tf_op | source)
XLA Modules:
  0.0 93.3 jit_solution(15246753200204464572)
XLA Ops:
  0.0 0.0 copy-start
  0.0 3.2 %collective-permute-start = (bf16[4096,512]{1,0:T(8,128)(2,1)}, bf16[4096,512]{1,0:T(8,128)(2,1)}, u32[]{:S(2)}, u32[]{:S(2)}) collective-permute-start(bf16[4096,512]{1,0:T(8,128)(2,1)} %own_ref.1), channel_id=1, source_target_pairs={{0,16},{16,0},{1,17},{17,1},{2,18},{18,2},{3,19},{19,3},{4,20},{20... | collective-permute-start | bytes 12582920 | tf_op jit(solution)/shard_map/ppermute | solution.py:156
  3.2 2.1 %pack.1 = bf16[16,34,4,128]{3,2,1,0:T(4,128)(2,1)} custom-call(s32[32,64]{1,0:T(8,128)} %bitcast.22, s32[16,64]{1,0:T(8,128)} %bitcast.23, bf16[64,8,4,128]{3,2,1,0:T(4,128)(2,1)} %bitcast.21), custom_call_target="tpu_custom_call" | custom-call | flops 1048576 | bytes 2097152 | tf_op jit(solution)/shard_map/pack/pallas_call | solution.py:158
  5.3 9.4 %all-to-all-start = ((bf16[16,34,4,128]{3,2,1,0:T(4,128)(2,1)}), bf16[16,34,4,128]{3,2,1,0:T(4,128)(2,1)S(1)}, u32[]{:S(2)}, u32[]{:S(2)}) async-start(bf16[16,34,4,128]{3,2,1,0:T(4,128)(2,1)} %pack.1), calls=%async_computation | async-start | bytes 1114112 | tf_op jit(solution)/shard_map/all_to_all | solution.py:175
  14.7 0.0 copy-done
  14.7 1.0 %fusion.2 = f32[512,512]{1,0:T(8,128)S(1)} fusion(f32[512,512]{1,0:T(8,128)S(1)} %copy-done), kind=kOutput, calls=%fused_computation.5 | convolution fusion | flops 805830656 | bytes 2097152 | tf_op jit(solution)/shard_map/dot_general | solution.py:178
  15.7 1.0 %fusion.1.early_ref = f32[512,512]{1,0:T(8,128)S(1)} fusion(f32[512,512]{1,0:T(8,128)S(1)} %fusion.2, f32[512,512]{1,0:T(8,128)S(1)} %copy-done), kind=kOutput, calls=%fused_computation.3 | convolution fusion | flops 805568512 | bytes 3145728 | tf_op jit(solution)/shard_map/dot_general | solution.py:179
  16.8 13.2 %all-to-all-done = bf16[16,34,4,128]{3,2,1,0:T(4,128)(2,1)S(1)} async-done(((bf16[16,34,4,128]{3,2,1,0:T(4,128)(2,1)}), bf16[16,34,4,128]{3,2,1,0:T(4,128)(2,1)S(1)}, u32[]{:S(2)}, u32[]{:S(2)}) %all-to-all-start) | async-done | bytes 557088 | tf_op jit(solution)/shard_map/all_to_all | solution.py:175
  29.9 0.0 collective-permute-done.other_ref
  29.9 7.3 %project.1 = f32[512,512]{1,0:T(8,128)S(1)} custom-call(s32[1]{0:T(128)} %bitcast.core_ref, bf16[16,136,128]{2,1,0:T(8,128)(2,1)S(1)} %bitcast.17, bf16[4096,512]{1,0:T(8,128)(2,1)} %own_ref.1, bf16[4096,512]{1,0:T(8,128)(2,1)} %collective-permute-done.other_ref, f32[512,512]{1,0:T(8,128)S(1)} %fusion.1.early_ref), custom_call_target="tpu_custom_call" | custom-call | flops 4294967296 | bytes 12582912 | tf_op jit(solution)/shard_map/project/pallas_call | solution.py:182
  37.3 0.1 multiply_convert_fusion
  37.4 16.3 %all_to_all.20 = f16[16,32,512]{2,1,0:T(8,128)(2,1)S(1)} all-to-all(f16[16,32,512]{2,1,0:T(8,128)(2,1)S(1)} %bitcast.20), channel_id=1, replica_groups=mesh['zh'=2,'x'=4,'c'=2,'zl'=4,'y'=4] {'y','x'}, dimensions={0} | all-to-all | bytes 1048576 | tf_op jit(solution)/shard_map/all_to_all | solution.py:205
  53.7 0.1 convert_reduce_fusion
  53.8 16.5 %all_to_all.21 = f16[8,32,512]{2,1,0:T(8,128)(2,1)S(1)} all-to-all(f16[8,32,512]{2,1,0:T(8,128)(2,1)S(1)} %broadcast_in_dim.4), channel_id=1, replica_groups=mesh['zh'=2,'x'=4,'c'=2,'zl'=4,'y'=4] {'zh','zl'}, dimensions={0} | all-to-all | bytes 524288 | tf_op jit(solution)/shard_map/all_to_all | solution.py:208
  70.4 13.0 %all_to_all.22 = f16[16,32,512]{2,1,0:T(8,128)(2,1)S(1)} all-to-all(f16[16,32,512]{2,1,0:T(8,128)(2,1)S(1)} %broadcast_in_dim.5), channel_id=1, replica_groups=mesh['zh'=2,'x'=4,'c'=2,'zl'=4,'y'=4] {'y','x'}, dimensions={0} | all-to-all | bytes 1048576 | tf_op jit(solution)/shard_map/all_to_all | solution.py:211
  83.4 0.1 convert_multiply_fusion
  83.6 1.0 %fusion = f32[512,512]{1,0:T(8,128)S(1)} fusion(f32[512,512]{1,0:T(8,128)S(1)} %bitcast.18, f32[512,512]{1,0:T(8,128)S(1)} %copy-done), kind=kOutput, calls=%fused_computation.1 | convolution fusion | flops 805830656 | bytes 3145728 | tf_op jit(solution)/shard_map/dot_general | solution.py:214
  84.6 1.0 %fusion.3 = f32[512,512]{1,0:T(8,128)S(1)} fusion(f32[512,512]{1,0:T(8,128)S(1)} %bitcast.19, f32[512,512]{1,0:T(8,128)S(1)} %fusion), kind=kOutput, calls=%fused_computation.12 | convolution fusion | flops 805306368 | bytes 3145728 | tf_op jit(solution)/shard_map/dot_general | solution.py:215
  85.6 4.0 %collective-permute-start.1 = (f32[512,512]{1,0:T(8,128)S(1)}, f32[512,512]{1,0:T(8,128)S(1)}, u32[]{:S(2)}, u32[]{:S(2)}) collective-permute-start(f32[512,512]{1,0:T(8,128)S(1)} %fusion.3), channel_id=1, source_target_pairs={{0,16},{16,0},{1,17},{17,1},{2,18},{18,2},{3,19},{19,3},{4,20},{20... | collective-permute-start | bytes 3145736 | tf_op jit(solution)/shard_map/ppermute | solution.py:216
  89.6 2.3 %collective-permute-done.1 = f32[512,512]{1,0:T(8,128)S(1)} collective-permute-done((f32[512,512]{1,0:T(8,128)S(1)}, f32[512,512]{1,0:T(8,128)S(1)}, u32[]{:S(2)}, u32[]{:S(2)}) %collective-permute-start.1) | collective-permute-done | bytes 1048608 | tf_op jit(solution)/shard_map/ppermute | solution.py:216
  91.9 1.3 %multiply_subtract_fusion = f32[512,512]{1,0:T(8,128)} fusion(f32[512,512]{1,0:T(8,128)S(1)} %fusion.1.early_ref, f32[512,512]{1,0:T(8,128)S(1)} %fusion.3, f32[512,512]{1,0:T(8,128)S(1)} %collective-permute-done.1), kind=kLoop, calls=%fused_computation.6 | loop fusion | flops 786432 | bytes 4194304 | tf_op jit(solution)/shard_map/sub | solution.py:216
  (5 shorter events, 0.1 us)
Async XLA Ops:
  0.0 14.7 %copy-start = (f32[512,512]{1,0:T(8,128)S(1)}, f32[512,512]{1,0:T(8,128)}, u32[]{:S(2)}) copy-start(f32[512,512]{1,0:T(8,128)} %param.9) | copy-start | bytes 3145732
  0.0 29.9 %collective-permute-start = (bf16[4096,512]{1,0:T(8,128)(2,1)}, bf16[4096,512]{1,0:T(8,128)(2,1)}, u32[]{:S(2)}, u32[]{:S(2)}) collective-permute-start(bf16[4096,512]{1,0:T(8,128)(2,1)} %own_ref.1), channel_id=1, source_target_pairs={{0,16},{16,0},{1,17},{17,1},{2,18},{18,2},{3,19},{19,3},{4,20},{20... | collective-permute-start | bytes 12582920 | tf_op jit(solution)/shard_map/ppermute | solution.py:156
  5.3 24.6 %all-to-all-start = ((bf16[16,34,4,128]{3,2,1,0:T(4,128)(2,1)}), bf16[16,34,4,128]{3,2,1,0:T(4,128)(2,1)S(1)}, u32[]{:S(2)}, u32[]{:S(2)}) async-start(bf16[16,34,4,128]{3,2,1,0:T(4,128)(2,1)} %pack.1), calls=%async_computation | async-start | bytes 1114112 | tf_op jit(solution)/shard_map/all_to_all | solution.py:175
  85.6 6.3 %collective-permute-start.1 = (f32[512,512]{1,0:T(8,128)S(1)}, f32[512,512]{1,0:T(8,128)S(1)}, u32[]{:S(2)}, u32[]{:S(2)}) collective-permute-start(f32[512,512]{1,0:T(8,128)S(1)} %fusion.3), channel_id=1, source_target_pairs={{0,16},{16,0},{1,17},{17,1},{2,18},{18,2},{3,19},{19,3},{4,20},{20... | collective-permute-start | bytes 3145736 | tf_op jit(solution)/shard_map/ppermute | solution.py:216

commit v7 on v6

--- a/solution.py
+++ b/solution.py
@@ -1,3 +1,4 @@
+import functools
 import math
 
 import jax
@@ -6,6 +7,7 @@
 from jax.experimental import pallas as pl
 from jax.experimental.pallas import tpu as pltpu
 from jax.sharding import Mesh, PartitionSpec as P
+
 
 penalty = 0.25
 term_scale = 256.0
@@ -131,6 +133,12 @@
         out_ref[...] = total
 
 
+def combine_kernel(scale, made_a, got_a, made_b, got_b, early_ref, out_ref):
+    share = made_a.shape[0]
+    out_ref[:share, :] = (made_a[...] + got_a[...]) * scale - early_ref[:share, :]
+    out_ref[share:, :] = (made_b[...] + got_b[...]) * scale - early_ref[share:, :]
+
+
 def to_half(values, scale):
     return (values * scale).astype(jnp.float16)
 
@@ -197,7 +205,7 @@
         name="project",
     )(core.astype(jnp.int32).reshape(1), moved, whitening, other, early)
 
-    plane_axes, column_axes = ("y", "x"), ("zh", "zl")
+    plane_axes, column_axes = ("y", "x"), ("zl", "zh")
     plane = lax.axis_size(plane_axes)
     column = lax.axis_size(column_axes)
     part = half // plane
@@ -212,8 +220,20 @@
     projected = from_half(got.reshape(half, topics), total_scale)
 
     scores = jnp.dot(projected, factors, precision=HIGH) * (1.0 / math.sqrt(topics))
-    moment = jnp.dot(projected.T, scores * scores, precision=HIGH)
-    return (moment + lax.ppermute(moment, "c", swap)) * (1.0 / (2 * half)) - early
+    squares = scores * scores
+    share = topics // 2
+    made, got = [], []
+    for k in range(2):
+        made.append(jnp.dot(projected[:, k * share:(k + 1) * share].T, squares, precision=HIGH))
+        got.append(lax.ppermute(made[k], "c", swap))
+    return pl.pallas_call(
+        functools.partial(combine_kernel, 1.0 / (2 * half)),
+        out_shape=jax.ShapeDtypeStruct((topics, topics), jnp.float32),
+        in_specs=[vmem] * 5,
+        out_specs=vmem,
+        compiler_params=pltpu.CompilerParams(vmem_limit_bytes=16 << 20),
+        name="combine",
+    )(made[0], got[0], made[1], got[1], early)
 
 
 def solution(mesh):

time: 93.6 us -> 92.3 us (0.986); the launches traced: 93.3 us -> 90.6 us
  blocking collectives: 45.8 us -> 42.6 us
  other arithmetic: 1.74 us -> 0.4 us
  Pallas kernels: 9.44 us -> 10.6 us
    all_to_all x1, blocking collectives: 16.5 us -> 14.2 us  [shards(): got = lax.all_to_all(sent, column_axes, 0, 0, tiled=True)]
    sub x1 -> x0, other arithmetic: 1.33 us -> none  [shards(): (moment + lax.ppermute(moment, 'c', swap)) * (1.0 / (2 * half)) - early]
    pallas_call x0 -> x1, Pallas kernels: none -> 1.12 us  [shards(): pl.pallas_call(functools.partial(combine_kernel, 1.0 / (2 * half)), out_s...]
    all_to_all x2, blocking collectives: 29.3 us -> 28.4 us  [shards(): got = lax.all_to_all(sent, plane_axes, 0, 0, tiled=True)]
    ppermute x1 -> x2, starting transfers between devices: 4.01 us -> 4.65 us  [shards(): got.append(lax.ppermute(made[k], 'c', swap))]
    ppermute x1 -> x2, waiting for transfers between devices: 2.29 us -> 2.19 us  [shards(): got.append(lax.ppermute(made[k], 'c', swap))]
  transfers between devices with their start and end apart: 3 -> 4, of which waited for: 2 -> 3; matrix products, arithmetic and copies ran while one was open for 2% -> 2% of each run, Pallas kernels for 2% -> 2%
where the time goes in v7:
time: 92.3 us; the launch traced here: 90.6 us
  blocking collectives  42.6 us (46%)
  starting transfers between devices  17.2 us (19%)
  waiting for transfers between devices  15.4 us (17%)
  Pallas kernels  10.6 us (11%)
  matrix products  4.29 us (5%)
    all_to_all x2, blocking collectives, shards(): got = lax.all_to_all(sent, plane_axes, 0, 0, tiled=True)  28.4 us
    all_to_all x1, blocking collectives, shards(): got = lax.all_to_all(sent, column_axes, 0, 0, tiled=True)  14.2 us
    all_to_all x1, waiting for transfers between devices, shards(): moved = lax.all_to_all(packed, doc_axes, 0, 0, tiled=True)  13.2 us
    all_to_all x1, starting transfers between devices, shards(): moved = lax.all_to_all(packed, doc_axes, 0, 0, tiled=True)  9.36 us
    pallas_call x1, Pallas kernels, shards(): pl.pallas_call(project_kernel, out_shape=jax.ShapeDtypeStruct((half, topi...  7.31 us
    ppermute x2, starting transfers between devices, shards(): got.append(lax.ppermute(made[k], 'c', swap))  4.65 us
    ppermute x1, starting transfers between devices, shards(): other = lax.ppermute(whitening, 'c', swap)  3.2 us
    ppermute x2, waiting for transfers between devices, shards(): got.append(lax.ppermute(made[k], 'c', swap))  2.19 us
  transfers between devices with their start and end apart: 4, of which 3 were waited for; matrix products, arithmetic and copies ran while one was open for 2% of the time, Pallas kernels for 2%

profile of v7, /device:TPU:1, one launch (start us, length us, event | category | flops | bytes accessed | tf_op | source)
XLA Modules:
  0.0 90.6 jit_solution(14639277866052278368)
XLA Ops:
  0.0 0.0 copy-start
  0.0 3.2 %collective-permute-start = (bf16[4096,512]{1,0:T(8,128)(2,1)}, bf16[4096,512]{1,0:T(8,128)(2,1)}, u32[]{:S(2)}, u32[]{:S(2)}) collective-permute-start(bf16[4096,512]{1,0:T(8,128)(2,1)} %own_ref.1), channel_id=1, source_target_pairs={{0,16},{16,0},{1,17},{17,1},{2,18},{18,2},{3,19},{19,3},{4,20},{20... | collective-permute-start | bytes 12582920 | tf_op jit(solution)/shard_map/ppermute | solution.py:164
  3.2 2.1 %pack.1 = bf16[16,34,4,128]{3,2,1,0:T(4,128)(2,1)} custom-call(s32[32,64]{1,0:T(8,128)} %bitcast.23, s32[16,64]{1,0:T(8,128)} %bitcast.24, bf16[64,8,4,128]{3,2,1,0:T(4,128)(2,1)} %bitcast.22), custom_call_target="tpu_custom_call" | custom-call | flops 1048576 | bytes 2097152 | tf_op jit(solution)/shard_map/pack/pallas_call | solution.py:166
  5.3 9.4 %all-to-all-start = ((bf16[16,34,4,128]{3,2,1,0:T(4,128)(2,1)}), bf16[16,34,4,128]{3,2,1,0:T(4,128)(2,1)S(1)}, u32[]{:S(2)}, u32[]{:S(2)}) async-start(bf16[16,34,4,128]{3,2,1,0:T(4,128)(2,1)} %pack.1), calls=%async_computation | async-start | bytes 1114112 | tf_op jit(solution)/shard_map/all_to_all | solution.py:183
  14.7 0.0 copy-done
  14.7 1.0 %fusion.2 = f32[512,512]{1,0:T(8,128)S(1)} fusion(f32[512,512]{1,0:T(8,128)S(1)} %copy-done), kind=kOutput, calls=%fused_computation.5 | convolution fusion | flops 805830656 | bytes 2097152 | tf_op jit(solution)/shard_map/dot_general | solution.py:186
  15.7 1.0 %fusion.1.early_ref = f32[512,512]{1,0:T(8,128)S(1)} fusion(f32[512,512]{1,0:T(8,128)S(1)} %fusion.2, f32[512,512]{1,0:T(8,128)S(1)} %copy-done), kind=kOutput, calls=%fused_computation.3 | convolution fusion | flops 805568512 | bytes 3145728 | tf_op jit(solution)/shard_map/dot_general | solution.py:187
  16.8 13.2 %all-to-all-done = bf16[16,34,4,128]{3,2,1,0:T(4,128)(2,1)S(1)} async-done(((bf16[16,34,4,128]{3,2,1,0:T(4,128)(2,1)}), bf16[16,34,4,128]{3,2,1,0:T(4,128)(2,1)S(1)}, u32[]{:S(2)}, u32[]{:S(2)}) %all-to-all-start) | async-done | bytes 557088 | tf_op jit(solution)/shard_map/all_to_all | solution.py:183
  29.9 0.0 collective-permute-done.other_ref
  29.9 7.3 %project.1 = f32[512,512]{1,0:T(8,128)S(1)} custom-call(s32[1]{0:T(128)} %bitcast.core_ref, bf16[16,136,128]{2,1,0:T(8,128)(2,1)S(1)} %bitcast.17, bf16[4096,512]{1,0:T(8,128)(2,1)} %own_ref.1, bf16[4096,512]{1,0:T(8,128)(2,1)} %collective-permute-done.other_ref, f32[512,512]{1,0:T(8,128)S(1)} %fusion.1.early_ref), custom_call_target="tpu_custom_call" | custom-call | flops 4294967296 | bytes 12582912 | tf_op jit(solution)/shard_map/project/pallas_call | solution.py:190
  37.3 0.1 multiply_convert_fusion
  37.4 16.3 %all_to_all.20 = f16[16,32,512]{2,1,0:T(8,128)(2,1)S(1)} all-to-all(f16[16,32,512]{2,1,0:T(8,128)(2,1)S(1)} %bitcast.21), channel_id=1, replica_groups=mesh['zh'=2,'x'=4,'c'=2,'zl'=4,'y'=4] {'y','x'}, dimensions={0} | all-to-all | bytes 1048576 | tf_op jit(solution)/shard_map/all_to_all | solution.py:213
  53.7 0.1 convert_reduce_fusion
  53.8 14.2 %all_to_all.21 = f16[8,32,512]{2,1,0:T(8,128)(2,1)S(1)} all-to-all(f16[8,32,512]{2,1,0:T(8,128)(2,1)S(1)} %broadcast_in_dim.4), channel_id=1, replica_groups=mesh['zh'=2,'x'=4,'c'=2,'zl'=4,'y'=4] {'zl','zh'}, dimensions={0} | all-to-all | bytes 524288 | tf_op jit(solution)/shard_map/all_to_all | solution.py:216
  68.2 12.1 %all_to_all.22 = f16[16,32,512]{2,1,0:T(8,128)(2,1)S(1)} all-to-all(f16[16,32,512]{2,1,0:T(8,128)(2,1)S(1)} %broadcast_in_dim.5), channel_id=1, replica_groups=mesh['zh'=2,'x'=4,'c'=2,'zl'=4,'y'=4] {'y','x'}, dimensions={0} | all-to-all | bytes 1048576 | tf_op jit(solution)/shard_map/all_to_all | solution.py:219
  80.2 0.1 convert_multiply_fusion
  80.4 1.0 %fusion = f32[512,512]{1,0:T(8,128)S(1)} fusion(f32[512,512]{1,0:T(8,128)S(1)} %bitcast.18, f32[512,512]{1,0:T(8,128)S(1)} %copy-done), kind=kOutput, calls=%fused_computation.1 | convolution fusion | flops 805830656 | bytes 3145728 | tf_op jit(solution)/shard_map/dot_general | solution.py:222
  81.4 0.6 fusion.3.made_b
  82.0 0.6 fusion.5.made_a
  82.6 4.6 %collective-permute-start.1 = (f32[256,512]{1,0:T(8,128)S(1)}, f32[256,512]{1,0:T(8,128)S(1)}, u32[]{:S(2)}, u32[]{:S(2)}) collective-permute-start(f32[256,512]{1,0:T(8,128)S(1)} %fusion.5.made_a), channel_id=1, source_target_pairs={{0,16},{16,0},{1,17},{17,1},{2,18},{18,2},{3,19},{19,3},{4,20},{20... | collective-permute-start | bytes 1572872 | tf_op jit(solution)/shard_map/ppermute | solution.py:228
  87.2 0.1 collective-permute-start.2
  87.3 1.4 %collective-permute-done.1.got_a = f32[256,512]{1,0:T(8,128)S(1)} collective-permute-done((f32[256,512]{1,0:T(8,128)S(1)}, f32[256,512]{1,0:T(8,128)S(1)}, u32[]{:S(2)}, u32[]{:S(2)}) %collective-permute-start.1) | collective-permute-done | bytes 524320 | tf_op jit(solution)/shard_map/ppermute | solution.py:228
  88.7 0.7 collective-permute-done.2.got_b
  89.5 1.1 %combine.1 = f32[512,512]{1,0:T(8,128)} custom-call(f32[256,512]{1,0:T(8,128)S(1)} %fusion.5.made_a, f32[256,512]{1,0:T(8,128)S(1)} %collective-permute-done.1.got_a, f32[256,512]{1,0:T(8,128)S(1)} %fusion.3.made_b, f32[256,512]{1,0:T(8,128)S(1)} %collective-permute-done.2.got_b, f32[512,512]{1,0:T(8,128)S(1)} %fusion.1.early_ref), custom_call_target="tpu_custom_call" | custom-call | tf_op jit(solution)/shard_map/combine/pallas_call | solution.py:229
  (5 shorter events, 0.1 us)
Async XLA Ops:
  0.0 14.7 %copy-start = (f32[512,512]{1,0:T(8,128)S(1)}, f32[512,512]{1,0:T(8,128)}, u32[]{:S(2)}) copy-start(f32[512,512]{1,0:T(8,128)} %param.9) | copy-start | bytes 3145732
  0.0 29.9 %collective-permute-start = (bf16[4096,512]{1,0:T(8,128)(2,1)}, bf16[4096,512]{1,0:T(8,128)(2,1)}, u32[]{:S(2)}, u32[]{:S(2)}) collective-permute-start(bf16[4096,512]{1,0:T(8,128)(2,1)} %own_ref.1), channel_id=1, source_target_pairs={{0,16},{16,0},{1,17},{17,1},{2,18},{18,2},{3,19},{19,3},{4,20},{20... | collective-permute-start | bytes 12582920 | tf_op jit(solution)/shard_map/ppermute | solution.py:164
  5.3 24.6 %all-to-all-start = ((bf16[16,34,4,128]{3,2,1,0:T(4,128)(2,1)}), bf16[16,34,4,128]{3,2,1,0:T(4,128)(2,1)S(1)}, u32[]{:S(2)}, u32[]{:S(2)}) async-start(bf16[16,34,4,128]{3,2,1,0:T(4,128)(2,1)} %pack.1), calls=%async_computation | async-start | bytes 1114112 | tf_op jit(solution)/shard_map/all_to_all | solution.py:183
  82.6 6.1 %collective-permute-start.1 = (f32[256,512]{1,0:T(8,128)S(1)}, f32[256,512]{1,0:T(8,128)S(1)}, u32[]{:S(2)}, u32[]{:S(2)}) collective-permute-start(f32[256,512]{1,0:T(8,128)S(1)} %fusion.5.made_a), channel_id=1, source_target_pairs={{0,16},{16,0},{1,17},{17,1},{2,18},{18,2},{3,19},{19,3},{4,20},{20... | collective-permute-start | bytes 1572872 | tf_op jit(solution)/shard_map/ppermute | solution.py:228
  87.2 2.3 %collective-permute-start.2 = (f32[256,512]{1,0:T(8,128)S(1)}, f32[256,512]{1,0:T(8,128)S(1)}, u32[]{:S(2)}, u32[]{:S(2)}) collective-permute-start(f32[256,512]{1,0:T(8,128)S(1)} %fusion.3.made_b), channel_id=1, source_target_pairs={{0,16},{16,0},{1,17},{17,1},{2,18},{18,2},{3,19},{19,3},{4,20},{20... | collective-permute-start | bytes 1572872 | tf_op jit(solution)/shard_map/ppermute | solution.py:228

commit v8 on v7

--- a/solution.py
+++ b/solution.py
@@ -30,8 +30,9 @@
     copies = []
     for target in range(targets):
         chip, core = target // 2, target % 2
+        place = core * chips + (chip % (chips // 2)) * 2 + chip // (chips // 2)
         copy = pltpu.make_async_copy(
-            counts_ref.at[pl.ds(core * docs, docs), chip], packed.at[target, pl.ds(0, docs)], in_sems.at[target])
+            counts_ref.at[pl.ds(core * docs, docs), chip], packed.at[place, pl.ds(0, docs)], in_sems.at[target])
         copy.start()
         copies.append(copy)
     for copy in small:
@@ -46,10 +47,11 @@
         rows = jnp.concatenate([m[:, core * docs:(core + 1) * docs] for m in marked], axis=1)
         for chip in range(chips):
             row = jnp.broadcast_to(rows[chip:chip + 1, :], (2 * group, width))
-            packed[chip * 2 + core, docs:docs + 2] = row.reshape(2, group, width).astype(packed.dtype)
+            packed[core * chips + (chip % (chips // 2)) * 2 + chip // (chips // 2), docs:docs + 2] = row.reshape(2, group, width).astype(packed.dtype)
     sends = []
+    for copy in copies:
+        copy.wait()
     for target in range(targets):
-        copies[target].wait()
         copy = pltpu.make_async_copy(packed.at[target], out_ref.at[target], out_sems.at[target])
         copy.start()
         sends.append(copy)
@@ -148,7 +150,7 @@
 
 
 def shards(counts, tile_index, tile_count, whitening, factors):
-    doc_axes = ("zh", "x", "c")
+    doc_axes = ('c', 'x', 'zh')
     doc_devices = lax.axis_size(doc_axes)
     chips = doc_devices // 2
     doc_local = counts.shape[0]

time: 92.3 us -> 90.5 us (0.980); the launches traced: 90.6 us -> 90.1 us
  waiting for transfers between devices: 15.4 us -> 13.6 us
  starting transfers between devices: 17.2 us -> 18.4 us
    all_to_all x1, waiting for transfers between devices: 13.2 us -> 11.4 us  [shards(): moved = lax.all_to_all(packed, doc_axes, 0, 0, tiled=True)]
    ppermute x2, starting transfers between devices: 4.65 us -> 5.89 us  [shards(): got.append(lax.ppermute(made[k], 'c', swap))]
where the time goes in v8:
time: 90.5 us; the launch traced here: 90.1 us
  blocking collectives  42.6 us (47%)
  starting transfers between devices  18.4 us (20%)
  waiting for transfers between devices  13.6 us (15%)
  Pallas kernels  10.6 us (12%)
  matrix products  4.28 us (5%)
    all_to_all x2, blocking collectives, shards(): got = lax.all_to_all(sent, plane_axes, 0, 0, tiled=True)  28.4 us
    all_to_all x1, blocking collectives, shards(): got = lax.all_to_all(sent, column_axes, 0, 0, tiled=True)  14.3 us
    all_to_all x1, waiting for transfers between devices, shards(): moved = lax.all_to_all(packed, doc_axes, 0, 0, tiled=True)  11.4 us
    all_to_all x1, starting transfers between devices, shards(): moved = lax.all_to_all(packed, doc_axes, 0, 0, tiled=True)  9.36 us
    pallas_call x1, Pallas kernels, shards(): pl.pallas_call(project_kernel, out_shape=jax.ShapeDtypeStruct((half, topi...  7.31 us
    ppermute x2, starting transfers between devices, shards(): got.append(lax.ppermute(made[k], 'c', swap))  5.89 us
    ppermute x1, starting transfers between devices, shards(): other = lax.ppermute(whitening, 'c', swap)  3.2 us
    ppermute x2, waiting for transfers between devices, shards(): got.append(lax.ppermute(made[k], 'c', swap))  2.19 us
  transfers between devices with their start and end apart: 4, of which 3 were waited for; matrix products, arithmetic and copies ran while one was open for 2% of the time, Pallas kernels for 2%

profile of v8, /device:TPU:1, one launch (start us, length us, event | category | flops | bytes accessed | tf_op | source)
XLA Modules:
  0.0 90.1 jit_solution(7909253592514252165)
XLA Ops:
  0.0 0.0 copy-start
  0.0 3.2 %collective-permute-start = (bf16[4096,512]{1,0:T(8,128)(2,1)}, bf16[4096,512]{1,0:T(8,128)(2,1)}, u32[]{:S(2)}, u32[]{:S(2)}) collective-permute-start(bf16[4096,512]{1,0:T(8,128)(2,1)} %own_ref.1), channel_id=1, source_target_pairs={{0,16},{16,0},{1,17},{17,1},{2,18},{18,2},{3,19},{19,3},{4,20},{20... | collective-permute-start | bytes 12582920 | tf_op jit(solution)/shard_map/ppermute | solution.py:166
  3.2 2.2 %pack.1 = bf16[16,34,4,128]{3,2,1,0:T(4,128)(2,1)} custom-call(s32[32,64]{1,0:T(8,128)} %bitcast.23, s32[16,64]{1,0:T(8,128)} %bitcast.24, bf16[64,8,4,128]{3,2,1,0:T(4,128)(2,1)} %bitcast.22), custom_call_target="tpu_custom_call" | custom-call | flops 1048576 | bytes 2097152 | tf_op jit(solution)/shard_map/pack/pallas_call | solution.py:168
  5.4 9.4 %all-to-all-start = ((bf16[16,34,4,128]{3,2,1,0:T(4,128)(2,1)}), bf16[16,34,4,128]{3,2,1,0:T(4,128)(2,1)S(1)}, u32[]{:S(2)}, u32[]{:S(2)}) async-start(bf16[16,34,4,128]{3,2,1,0:T(4,128)(2,1)} %pack.1), calls=%async_computation | async-start | bytes 1114112 | tf_op jit(solution)/shard_map/all_to_all | solution.py:185
  14.7 0.0 copy-done
  14.7 1.0 %fusion.2 = f32[512,512]{1,0:T(8,128)S(1)} fusion(f32[512,512]{1,0:T(8,128)S(1)} %copy-done), kind=kOutput, calls=%fused_computation.5 | convolution fusion | flops 805830656 | bytes 2097152 | tf_op jit(solution)/shard_map/dot_general | solution.py:188
  15.8 1.0 %fusion.1.early_ref = f32[512,512]{1,0:T(8,128)S(1)} fusion(f32[512,512]{1,0:T(8,128)S(1)} %fusion.2, f32[512,512]{1,0:T(8,128)S(1)} %copy-done), kind=kOutput, calls=%fused_computation.3 | convolution fusion | flops 805568512 | bytes 3145728 | tf_op jit(solution)/shard_map/dot_general | solution.py:189
  16.8 11.4 %all-to-all-done = bf16[16,34,4,128]{3,2,1,0:T(4,128)(2,1)S(1)} async-done(((bf16[16,34,4,128]{3,2,1,0:T(4,128)(2,1)}), bf16[16,34,4,128]{3,2,1,0:T(4,128)(2,1)S(1)}, u32[]{:S(2)}, u32[]{:S(2)}) %all-to-all-start) | async-done | bytes 557088 | tf_op jit(solution)/shard_map/all_to_all | solution.py:185
  28.2 0.0 collective-permute-done.other_ref
  28.2 7.3 %project.1 = f32[512,512]{1,0:T(8,128)S(1)} custom-call(s32[1]{0:T(128)} %bitcast.core_ref, bf16[16,136,128]{2,1,0:T(8,128)(2,1)S(1)} %bitcast.17, bf16[4096,512]{1,0:T(8,128)(2,1)} %own_ref.1, bf16[4096,512]{1,0:T(8,128)(2,1)} %collective-permute-done.other_ref, f32[512,512]{1,0:T(8,128)S(1)} %fusion.1.early_ref), custom_call_target="tpu_custom_call" | custom-call | flops 4294967296 | bytes 12582912 | tf_op jit(solution)/shard_map/project/pallas_call | solution.py:192
  35.5 0.1 multiply_convert_fusion
  35.7 16.3 %all_to_all.20 = f16[16,32,512]{2,1,0:T(8,128)(2,1)S(1)} all-to-all(f16[16,32,512]{2,1,0:T(8,128)(2,1)S(1)} %bitcast.21), channel_id=1, replica_groups=mesh['zh'=2,'x'=4,'c'=2,'zl'=4,'y'=4] {'y','x'}, dimensions={0} | all-to-all | bytes 1048576 | tf_op jit(solution)/shard_map/all_to_all | solution.py:215
  52.0 0.1 convert_reduce_fusion
  52.1 14.3 %all_to_all.21 = f16[8,32,512]{2,1,0:T(8,128)(2,1)S(1)} all-to-all(f16[8,32,512]{2,1,0:T(8,128)(2,1)S(1)} %broadcast_in_dim.4), channel_id=1, replica_groups=mesh['zh'=2,'x'=4,'c'=2,'zl'=4,'y'=4] {'zl','zh'}, dimensions={0} | all-to-all | bytes 524288 | tf_op jit(solution)/shard_map/all_to_all | solution.py:218
  66.5 12.0 %all_to_all.22 = f16[16,32,512]{2,1,0:T(8,128)(2,1)S(1)} all-to-all(f16[16,32,512]{2,1,0:T(8,128)(2,1)S(1)} %broadcast_in_dim.5), channel_id=1, replica_groups=mesh['zh'=2,'x'=4,'c'=2,'zl'=4,'y'=4] {'y','x'}, dimensions={0} | all-to-all | bytes 1048576 | tf_op jit(solution)/shard_map/all_to_all | solution.py:221
  78.5 0.1 convert_multiply_fusion
  78.7 1.0 %fusion = f32[512,512]{1,0:T(8,128)S(1)} fusion(f32[512,512]{1,0:T(8,128)S(1)} %bitcast.18, f32[512,512]{1,0:T(8,128)S(1)} %copy-done), kind=kOutput, calls=%fused_computation.1 | convolution fusion | flops 805830656 | bytes 3145728 | tf_op jit(solution)/shard_map/dot_general | solution.py:224
  79.7 0.6 fusion.3.made_b
  80.3 0.6 fusion.5.made_a
  80.9 5.8 %collective-permute-start.1 = (f32[256,512]{1,0:T(8,128)S(1)}, f32[256,512]{1,0:T(8,128)S(1)}, u32[]{:S(2)}, u32[]{:S(2)}) collective-permute-start(f32[256,512]{1,0:T(8,128)S(1)} %fusion.5.made_a), channel_id=1, source_target_pairs={{0,16},{16,0},{1,17},{17,1},{2,18},{18,2},{3,19},{19,3},{4,20},{20... | collective-permute-start | bytes 1572872 | tf_op jit(solution)/shard_map/ppermute | solution.py:230
  86.7 0.1 collective-permute-start.2
  86.8 1.4 %collective-permute-done.1.got_a = f32[256,512]{1,0:T(8,128)S(1)} collective-permute-done((f32[256,512]{1,0:T(8,128)S(1)}, f32[256,512]{1,0:T(8,128)S(1)}, u32[]{:S(2)}, u32[]{:S(2)}) %collective-permute-start.1) | collective-permute-done | bytes 524320 | tf_op jit(solution)/shard_map/ppermute | solution.py:230
  88.3 0.7 collective-permute-done.2.got_b
  89.0 1.1 %combine.1 = f32[512,512]{1,0:T(8,128)} custom-call(f32[256,512]{1,0:T(8,128)S(1)} %fusion.5.made_a, f32[256,512]{1,0:T(8,128)S(1)} %collective-permute-done.1.got_a, f32[256,512]{1,0:T(8,128)S(1)} %fusion.3.made_b, f32[256,512]{1,0:T(8,128)S(1)} %collective-permute-done.2.got_b, f32[512,512]{1,0:T(8,128)S(1)} %fusion.1.early_ref), custom_call_target="tpu_custom_call" | custom-call | tf_op jit(solution)/shard_map/combine/pallas_call | solution.py:231
  (5 shorter events, 0.1 us)
Async XLA Ops:
  0.0 14.7 %copy-start = (f32[512,512]{1,0:T(8,128)S(1)}, f32[512,512]{1,0:T(8,128)}, u32[]{:S(2)}) copy-start(f32[512,512]{1,0:T(8,128)} %param.9) | copy-start | bytes 3145732
  0.0 28.2 %collective-permute-start = (bf16[4096,512]{1,0:T(8,128)(2,1)}, bf16[4096,512]{1,0:T(8,128)(2,1)}, u32[]{:S(2)}, u32[]{:S(2)}) collective-permute-start(bf16[4096,512]{1,0:T(8,128)(2,1)} %own_ref.1), channel_id=1, source_target_pairs={{0,16},{16,0},{1,17},{17,1},{2,18},{18,2},{3,19},{19,3},{4,20},{20... | collective-permute-start | bytes 12582920 | tf_op jit(solution)/shard_map/ppermute | solution.py:166
  5.4 22.8 %all-to-all-start = ((bf16[16,34,4,128]{3,2,1,0:T(4,128)(2,1)}), bf16[16,34,4,128]{3,2,1,0:T(4,128)(2,1)S(1)}, u32[]{:S(2)}, u32[]{:S(2)}) async-start(bf16[16,34,4,128]{3,2,1,0:T(4,128)(2,1)} %pack.1), calls=%async_computation | async-start | bytes 1114112 | tf_op jit(solution)/shard_map/all_to_all | solution.py:185
  80.9 7.3 %collective-permute-start.1 = (f32[256,512]{1,0:T(8,128)S(1)}, f32[256,512]{1,0:T(8,128)S(1)}, u32[]{:S(2)}, u32[]{:S(2)}) collective-permute-start(f32[256,512]{1,0:T(8,128)S(1)} %fusion.5.made_a), channel_id=1, source_target_pairs={{0,16},{16,0},{1,17},{17,1},{2,18},{18,2},{3,19},{19,3},{4,20},{20... | collective-permute-start | bytes 1572872 | tf_op jit(solution)/shard_map/ppermute | solution.py:230
  86.7 2.3 %collective-permute-start.2 = (f32[256,512]{1,0:T(8,128)S(1)}, f32[256,512]{1,0:T(8,128)S(1)}, u32[]{:S(2)}, u32[]{:S(2)}) collective-permute-start(f32[256,512]{1,0:T(8,128)S(1)} %fusion.3.made_b), channel_id=1, source_target_pairs={{0,16},{16,0},{1,17},{17,1},{2,18},{18,2},{3,19},{19,3},{4,20},{20... | collective-permute-start | bytes 1572872 | tf_op jit(solution)/shard_map/ppermute | solution.py:230

commit v9 on v8

--- a/solution.py
+++ b/solution.py
@@ -13,7 +13,7 @@
 term_scale = 256.0
 total_scale = 4.0
 HIGH = lax.Precision.HIGH
-STEPS = 4
+STEPS = 2
 AHEAD = 2
 
 
@@ -32,9 +32,9 @@
         chip, core = target // 2, target % 2
         place = core * chips + (chip % (chips // 2)) * 2 + chip // (chips // 2)
         copy = pltpu.make_async_copy(
-            counts_ref.at[pl.ds(core * docs, docs), chip], packed.at[place, pl.ds(0, docs)], in_sems.at[target])
+            counts_ref.at[pl.ds(core * docs, docs), chip], packed.at[place, pl.ds(0, docs)], in_sems.at[place])
         copy.start()
-        copies.append(copy)
+        copies.append((place, copy))
     for copy in small:
         copy.wait()
     slots = group // 2
@@ -49,10 +49,9 @@
             row = jnp.broadcast_to(rows[chip:chip + 1, :], (2 * group, width))
             packed[core * chips + (chip % (chips // 2)) * 2 + chip // (chips // 2), docs:docs + 2] = row.reshape(2, group, width).astype(packed.dtype)
     sends = []
-    for copy in copies:
+    for place, copy in copies:
         copy.wait()
-    for target in range(targets):
-        copy = pltpu.make_async_copy(packed.at[target], out_ref.at[target], out_sems.at[target])
+        copy = pltpu.make_async_copy(packed.at[place], out_ref.at[place], out_sems.at[place])
         copy.start()
         sends.append(copy)
     for copy in sends:

time: 90.5 us -> 90.1 us (level)
  no operation moved by 1% of the time
where the time goes in v9:
time: 90.1 us; the launch traced here: 89.7 us
  blocking collectives  42.6 us (47%)
  starting transfers between devices  18.4 us (20%)
  waiting for transfers between devices  13.6 us (15%)
  Pallas kernels  10.2 us (11%)
  matrix products  4.29 us (5%)
    all_to_all x2, blocking collectives, shards(): got = lax.all_to_all(sent, plane_axes, 0, 0, tiled=True)  28.4 us
    all_to_all x1, blocking collectives, shards(): got = lax.all_to_all(sent, column_axes, 0, 0, tiled=True)  14.3 us
    all_to_all x1, waiting for transfers between devices, shards(): moved = lax.all_to_all(packed, doc_axes, 0, 0, tiled=True)  11.4 us
    all_to_all x1, starting transfers between devices, shards(): moved = lax.all_to_all(packed, doc_axes, 0, 0, tiled=True)  9.36 us
    pallas_call x1, Pallas kernels, shards(): pl.pallas_call(project_kernel, out_shape=jax.ShapeDtypeStruct((half, topi...  6.92 us
    ppermute x2, starting transfers between devices, shards(): got.append(lax.ppermute(made[k], 'c', swap))  5.89 us
    ppermute x1, starting transfers between devices, shards(): other = lax.ppermute(whitening, 'c', swap)  3.2 us
    ppermute x2, waiting for transfers between devices, shards(): got.append(lax.ppermute(made[k], 'c', swap))  2.19 us
  transfers between devices with their start and end apart: 4, of which 3 were waited for; matrix products, arithmetic and copies ran while one was open for 2% of the time, Pallas kernels for 2%

profile of v9, /device:TPU:1, one launch (start us, length us, event | category | flops | bytes accessed | tf_op | source)
XLA Modules:
  0.0 89.7 jit_solution(11189929161644080871)
XLA Ops:
  0.0 0.0 copy-start
  0.0 3.2 %collective-permute-start = (bf16[4096,512]{1,0:T(8,128)(2,1)}, bf16[4096,512]{1,0:T(8,128)(2,1)}, u32[]{:S(2)}, u32[]{:S(2)}) collective-permute-start(bf16[4096,512]{1,0:T(8,128)(2,1)} %own_ref.1), channel_id=1, source_target_pairs={{0,16},{16,0},{1,17},{17,1},{2,18},{18,2},{3,19},{19,3},{4,20},{20... | collective-permute-start | bytes 12582920 | tf_op jit(solution)/shard_map/ppermute | solution.py:165
  3.2 2.1 %pack.1 = bf16[16,34,4,128]{3,2,1,0:T(4,128)(2,1)} custom-call(s32[32,64]{1,0:T(8,128)} %bitcast.23, s32[16,64]{1,0:T(8,128)} %bitcast.24, bf16[64,8,4,128]{3,2,1,0:T(4,128)(2,1)} %bitcast.22), custom_call_target="tpu_custom_call" | custom-call | flops 1048576 | bytes 2097152 | tf_op jit(solution)/shard_map/pack/pallas_call | solution.py:167
  5.3 9.4 %all-to-all-start = ((bf16[16,34,4,128]{3,2,1,0:T(4,128)(2,1)}), bf16[16,34,4,128]{3,2,1,0:T(4,128)(2,1)S(1)}, u32[]{:S(2)}, u32[]{:S(2)}) async-start(bf16[16,34,4,128]{3,2,1,0:T(4,128)(2,1)} %pack.1), calls=%async_computation | async-start | bytes 1114112 | tf_op jit(solution)/shard_map/all_to_all | solution.py:184
  14.7 0.0 copy-done
  14.7 1.0 %fusion.2 = f32[512,512]{1,0:T(8,128)S(1)} fusion(f32[512,512]{1,0:T(8,128)S(1)} %copy-done), kind=kOutput, calls=%fused_computation.5 | convolution fusion | flops 805830656 | bytes 2097152 | tf_op jit(solution)/shard_map/dot_general | solution.py:187
  15.7 1.0 %fusion.1.early_ref = f32[512,512]{1,0:T(8,128)S(1)} fusion(f32[512,512]{1,0:T(8,128)S(1)} %fusion.2, f32[512,512]{1,0:T(8,128)S(1)} %copy-done), kind=kOutput, calls=%fused_computation.3 | convolution fusion | flops 805568512 | bytes 3145728 | tf_op jit(solution)/shard_map/dot_general | solution.py:188
  16.8 11.4 %all-to-all-done = bf16[16,34,4,128]{3,2,1,0:T(4,128)(2,1)S(1)} async-done(((bf16[16,34,4,128]{3,2,1,0:T(4,128)(2,1)}), bf16[16,34,4,128]{3,2,1,0:T(4,128)(2,1)S(1)}, u32[]{:S(2)}, u32[]{:S(2)}) %all-to-all-start) | async-done | bytes 557088 | tf_op jit(solution)/shard_map/all_to_all | solution.py:184
  28.2 0.0 collective-permute-done.other_ref
  28.2 6.9 %project.1 = f32[512,512]{1,0:T(8,128)S(1)} custom-call(s32[1]{0:T(128)} %bitcast.core_ref, bf16[16,136,128]{2,1,0:T(8,128)(2,1)S(1)} %bitcast.17, bf16[4096,512]{1,0:T(8,128)(2,1)} %own_ref.1, bf16[4096,512]{1,0:T(8,128)(2,1)} %collective-permute-done.other_ref, f32[512,512]{1,0:T(8,128)S(1)} %fusion.1.early_ref), custom_call_target="tpu_custom_call" | custom-call | flops 4294967296 | bytes 12582912 | tf_op jit(solution)/shard_map/project/pallas_call | solution.py:191
  35.1 0.1 multiply_convert_fusion
  35.3 16.3 %all_to_all.20 = f16[16,32,512]{2,1,0:T(8,128)(2,1)S(1)} all-to-all(f16[16,32,512]{2,1,0:T(8,128)(2,1)S(1)} %bitcast.21), channel_id=1, replica_groups=mesh['zh'=2,'x'=4,'c'=2,'zl'=4,'y'=4] {'y','x'}, dimensions={0} | all-to-all | bytes 1048576 | tf_op jit(solution)/shard_map/all_to_all | solution.py:214
  51.6 0.1 convert_reduce_fusion
  51.7 14.3 %all_to_all.21 = f16[8,32,512]{2,1,0:T(8,128)(2,1)S(1)} all-to-all(f16[8,32,512]{2,1,0:T(8,128)(2,1)S(1)} %broadcast_in_dim.4), channel_id=1, replica_groups=mesh['zh'=2,'x'=4,'c'=2,'zl'=4,'y'=4] {'zl','zh'}, dimensions={0} | all-to-all | bytes 524288 | tf_op jit(solution)/shard_map/all_to_all | solution.py:217
  66.1 12.0 %all_to_all.22 = f16[16,32,512]{2,1,0:T(8,128)(2,1)S(1)} all-to-all(f16[16,32,512]{2,1,0:T(8,128)(2,1)S(1)} %broadcast_in_dim.5), channel_id=1, replica_groups=mesh['zh'=2,'x'=4,'c'=2,'zl'=4,'y'=4] {'y','x'}, dimensions={0} | all-to-all | bytes 1048576 | tf_op jit(solution)/shard_map/all_to_all | solution.py:220
  78.1 0.1 convert_multiply_fusion
  78.3 1.0 %fusion = f32[512,512]{1,0:T(8,128)S(1)} fusion(f32[512,512]{1,0:T(8,128)S(1)} %bitcast.18, f32[512,512]{1,0:T(8,128)S(1)} %copy-done), kind=kOutput, calls=%fused_computation.1 | convolution fusion | flops 805830656 | bytes 3145728 | tf_op jit(solution)/shard_map/dot_general | solution.py:223
  79.3 0.6 fusion.3.made_b
  79.9 0.6 fusion.5.made_a
  80.5 5.8 %collective-permute-start.1 = (f32[256,512]{1,0:T(8,128)S(1)}, f32[256,512]{1,0:T(8,128)S(1)}, u32[]{:S(2)}, u32[]{:S(2)}) collective-permute-start(f32[256,512]{1,0:T(8,128)S(1)} %fusion.5.made_a), channel_id=1, source_target_pairs={{0,16},{16,0},{1,17},{17,1},{2,18},{18,2},{3,19},{19,3},{4,20},{20... | collective-permute-start | bytes 1572872 | tf_op jit(solution)/shard_map/ppermute | solution.py:229
  86.3 0.1 collective-permute-start.2
  86.4 1.4 %collective-permute-done.1.got_a = f32[256,512]{1,0:T(8,128)S(1)} collective-permute-done((f32[256,512]{1,0:T(8,128)S(1)}, f32[256,512]{1,0:T(8,128)S(1)}, u32[]{:S(2)}, u32[]{:S(2)}) %collective-permute-start.1) | collective-permute-done | bytes 524320 | tf_op jit(solution)/shard_map/ppermute | solution.py:229
  87.9 0.7 collective-permute-done.2.got_b
  88.6 1.1 %combine.1 = f32[512,512]{1,0:T(8,128)} custom-call(f32[256,512]{1,0:T(8,128)S(1)} %fusion.5.made_a, f32[256,512]{1,0:T(8,128)S(1)} %collective-permute-done.1.got_a, f32[256,512]{1,0:T(8,128)S(1)} %fusion.3.made_b, f32[256,512]{1,0:T(8,128)S(1)} %collective-permute-done.2.got_b, f32[512,512]{1,0:T(8,128)S(1)} %fusion.1.early_ref), custom_call_target="tpu_custom_call" | custom-call | tf_op jit(solution)/shard_map/combine/pallas_call | solution.py:230
  (5 shorter events, 0.1 us)
Async XLA Ops:
  0.0 14.7 %copy-start = (f32[512,512]{1,0:T(8,128)S(1)}, f32[512,512]{1,0:T(8,128)}, u32[]{:S(2)}) copy-start(f32[512,512]{1,0:T(8,128)} %param.9) | copy-start | bytes 3145732
  0.0 28.2 %collective-permute-start = (bf16[4096,512]{1,0:T(8,128)(2,1)}, bf16[4096,512]{1,0:T(8,128)(2,1)}, u32[]{:S(2)}, u32[]{:S(2)}) collective-permute-start(bf16[4096,512]{1,0:T(8,128)(2,1)} %own_ref.1), channel_id=1, source_target_pairs={{0,16},{16,0},{1,17},{17,1},{2,18},{18,2},{3,19},{19,3},{4,20},{20... | collective-permute-start | bytes 12582920 | tf_op jit(solution)/shard_map/ppermute | solution.py:165
  5.3 22.8 %all-to-all-start = ((bf16[16,34,4,128]{3,2,1,0:T(4,128)(2,1)}), bf16[16,34,4,128]{3,2,1,0:T(4,128)(2,1)S(1)}, u32[]{:S(2)}, u32[]{:S(2)}) async-start(bf16[16,34,4,128]{3,2,1,0:T(4,128)(2,1)} %pack.1), calls=%async_computation | async-start | bytes 1114112 | tf_op jit(solution)/shard_map/all_to_all | solution.py:184
  80.5 7.3 %collective-permute-start.1 = (f32[256,512]{1,0:T(8,128)S(1)}, f32[256,512]{1,0:T(8,128)S(1)}, u32[]{:S(2)}, u32[]{:S(2)}) collective-permute-start(f32[256,512]{1,0:T(8,128)S(1)} %fusion.5.made_a), channel_id=1, source_target_pairs={{0,16},{16,0},{1,17},{17,1},{2,18},{18,2},{3,19},{19,3},{4,20},{20... | collective-permute-start | bytes 1572872 | tf_op jit(solution)/shard_map/ppermute | solution.py:229
  86.3 2.3 %collective-permute-start.2 = (f32[256,512]{1,0:T(8,128)S(1)}, f32[256,512]{1,0:T(8,128)S(1)}, u32[]{:S(2)}, u32[]{:S(2)}) collective-permute-start(f32[256,512]{1,0:T(8,128)S(1)} %fusion.3.made_b), channel_id=1, source_target_pairs={{0,16},{16,0},{1,17},{17,1},{2,18},{18,2},{3,19},{19,3},{4,20},{20... | collective-permute-start | bytes 1572872 | tf_op jit(solution)/shard_map/ppermute | solution.py:229

commit v10 on v9

--- a/solution.py
+++ b/solution.py
@@ -13,7 +13,7 @@
 term_scale = 256.0
 total_scale = 4.0
 HIGH = lax.Precision.HIGH
-STEPS = 2
+STEPS = 1
 AHEAD = 2
 
 
@@ -65,13 +65,15 @@
     data = rows - 2 * group
     docs = data // group
     depth = own_ref.shape[0] // STEPS
-
-    def fetch(source, step):
+    unit = depth // 2
+    units = 4 * STEPS
+
+    def fetch(source, k):
         pltpu.make_async_copy(
-            source.at[pl.ds(lax.rem(step, STEPS) * depth, depth)], weights.at[step], sems.at[step]).start()
-
-    for step in range(AHEAD):
-        fetch(own_ref, jnp.int32(step))
+            source.at[pl.ds(lax.rem(k, units // 2) * unit, unit)], weights.at[k], sems.at[k]).start()
+
+    for k in range(AHEAD):
+        fetch(own_ref, jnp.int32(k))
 
     sub = lax.broadcasted_iota(jnp.int32, (8, width), 0)
     halves = []
@@ -107,20 +109,22 @@
 
     @pl.loop(0, 2 * STEPS)
     def _(step):
-        pltpu.make_async_copy(own_ref.at[pl.ds(0, depth)], weights.at[step], sems.at[step]).wait()
-
-        @pl.when(step + AHEAD < STEPS)
-        def _():
-            fetch(own_ref, step + AHEAD)
-
-        @pl.when(jnp.logical_and(step + AHEAD >= STEPS, step + AHEAD < 2 * STEPS))
-        def _():
-            fetch(other_ref, step + AHEAD)
-
         block = jnp.where(step < STEPS, core, 1 - core)
         base = (lax.rem(step, STEPS) * tiles_step).astype(jnp.float32)
         total = out_ref[...]
         for chunk in range(tiles_step // 2):
+            k = step * 2 + chunk // (tiles_step // 4)
+            if chunk % (tiles_step // 4) == 0:
+                pltpu.make_async_copy(own_ref.at[pl.ds(0, unit)], weights.at[k], sems.at[k]).wait()
+
+                @pl.when(k + AHEAD < units // 2)
+                def _():
+                    fetch(own_ref, k + AHEAD)
+
+                @pl.when(jnp.logical_and(k + AHEAD >= units // 2, k + AHEAD < units))
+                def _():
+                    fetch(other_ref, k + AHEAD)
+
             parts = []
             for t in (2 * chunk, 2 * chunk + 1):
                 mark = jnp.full((1, width), base + t, jnp.float32).astype(jnp.bfloat16)
@@ -129,7 +133,7 @@
                     jnp.where(tiles[block * 2 + 1] == mark, values[block * 2 + 1], jnp.zeros((), jnp.bfloat16))))
             dense = jnp.concatenate(parts, axis=1)
             total = total + jnp.dot(
-                dense, weights[step, 2 * chunk * width:2 * (chunk + 1) * width, :],
+                dense, weights[k, 2 * chunk * width % unit:2 * chunk * width % unit + 2 * width, :],
                 preferred_element_type=jnp.float32)
         out_ref[...] = total
 
@@ -194,11 +198,11 @@
         in_specs=[pl.BlockSpec(memory_space=pltpu.SMEM), vmem, anywhere, anywhere, anywhere],
         out_specs=vmem,
         scratch_shapes=[
-            pltpu.VMEM((2 * STEPS, depth, topics), jnp.bfloat16),
+            pltpu.VMEM((4 * STEPS, depth // 2, topics), jnp.bfloat16),
             pltpu.VMEM((half * group, width), jnp.float32),
             pltpu.VMEM((group, half, width), jnp.bfloat16),
             pltpu.VMEM((group, half, width), jnp.bfloat16),
-            pltpu.SemaphoreType.DMA((2 * STEPS,)),
+            pltpu.SemaphoreType.DMA((4 * STEPS,)),
         ],
         compiler_params=pltpu.CompilerParams(vmem_limit_bytes=50 << 20),
         cost_estimate=pl.CostEstimate(

time: 90.1 us -> 89.9 us (level)
  no operation moved by 1% of the time
where the time goes in v10:
time: 89.9 us; the launch traced here: 89.6 us
  blocking collectives  42.6 us (47%)
  starting transfers between devices  18.4 us (20%)
  waiting for transfers between devices  13.6 us (15%)
  Pallas kernels  10 us (11%)
  matrix products  4.29 us (5%)
    all_to_all x2, blocking collectives, shards(): got = lax.all_to_all(sent, plane_axes, 0, 0, tiled=True)  28.4 us
    all_to_all x1, blocking collectives, shards(): got = lax.all_to_all(sent, column_axes, 0, 0, tiled=True)  14.3 us
    all_to_all x1, waiting for transfers between devices, shards(): moved = lax.all_to_all(packed, doc_axes, 0, 0, tiled=True)  11.4 us
    all_to_all x1, starting transfers between devices, shards(): moved = lax.all_to_all(packed, doc_axes, 0, 0, tiled=True)  9.36 us
    pallas_call x1, Pallas kernels, shards(): pl.pallas_call(project_kernel, out_shape=jax.ShapeDtypeStruct((half, topi...  6.75 us
    ppermute x2, starting transfers between devices, shards(): got.append(lax.ppermute(made[k], 'c', swap))  5.89 us
    ppermute x1, starting transfers between devices, shards(): other = lax.ppermute(whitening, 'c', swap)  3.2 us
    ppermute x2, waiting for transfers between devices, shards(): got.append(lax.ppermute(made[k], 'c', swap))  2.19 us
  transfers between devices with their start and end apart: 4, of which 3 were waited for; matrix products, arithmetic and copies ran while one was open for 2% of the time, Pallas kernels for 2%

profile of v10, /device:TPU:1, one launch (start us, length us, event | category | flops | bytes accessed | tf_op | source)
XLA Modules:
  0.0 89.6 jit_solution(2490351518109566533)
XLA Ops:
  0.0 0.0 copy-start
  0.0 3.2 %collective-permute-start = (bf16[4096,512]{1,0:T(8,128)(2,1)}, bf16[4096,512]{1,0:T(8,128)(2,1)}, u32[]{:S(2)}, u32[]{:S(2)}) collective-permute-start(bf16[4096,512]{1,0:T(8,128)(2,1)} %own_ref.1), channel_id=1, source_target_pairs={{0,16},{16,0},{1,17},{17,1},{2,18},{18,2},{3,19},{19,3},{4,20},{20... | collective-permute-start | bytes 12582920 | tf_op jit(solution)/shard_map/ppermute | solution.py:169
  3.2 2.1 %pack.1 = bf16[16,34,4,128]{3,2,1,0:T(4,128)(2,1)} custom-call(s32[32,64]{1,0:T(8,128)} %bitcast.23, s32[16,64]{1,0:T(8,128)} %bitcast.24, bf16[64,8,4,128]{3,2,1,0:T(4,128)(2,1)} %bitcast.22), custom_call_target="tpu_custom_call" | custom-call | flops 1048576 | bytes 2097152 | tf_op jit(solution)/shard_map/pack/pallas_call | solution.py:171
  5.3 9.4 %all-to-all-start = ((bf16[16,34,4,128]{3,2,1,0:T(4,128)(2,1)}), bf16[16,34,4,128]{3,2,1,0:T(4,128)(2,1)S(1)}, u32[]{:S(2)}, u32[]{:S(2)}) async-start(bf16[16,34,4,128]{3,2,1,0:T(4,128)(2,1)} %pack.1), calls=%async_computation | async-start | bytes 1114112 | tf_op jit(solution)/shard_map/all_to_all | solution.py:188
  14.7 0.0 copy-done
  14.7 1.0 %fusion.2 = f32[512,512]{1,0:T(8,128)S(1)} fusion(f32[512,512]{1,0:T(8,128)S(1)} %copy-done), kind=kOutput, calls=%fused_computation.5 | convolution fusion | flops 805830656 | bytes 2097152 | tf_op jit(solution)/shard_map/dot_general | solution.py:191
  15.7 1.0 %fusion.1.early_ref = f32[512,512]{1,0:T(8,128)S(1)} fusion(f32[512,512]{1,0:T(8,128)S(1)} %fusion.2, f32[512,512]{1,0:T(8,128)S(1)} %copy-done), kind=kOutput, calls=%fused_computation.3 | convolution fusion | flops 805568512 | bytes 3145728 | tf_op jit(solution)/shard_map/dot_general | solution.py:192
  16.8 11.4 %all-to-all-done = bf16[16,34,4,128]{3,2,1,0:T(4,128)(2,1)S(1)} async-done(((bf16[16,34,4,128]{3,2,1,0:T(4,128)(2,1)}), bf16[16,34,4,128]{3,2,1,0:T(4,128)(2,1)S(1)}, u32[]{:S(2)}, u32[]{:S(2)}) %all-to-all-start) | async-done | bytes 557088 | tf_op jit(solution)/shard_map/all_to_all | solution.py:188
  28.2 0.0 collective-permute-done.other_ref
  28.2 6.8 %project.1 = f32[512,512]{1,0:T(8,128)S(1)} custom-call(s32[1]{0:T(128)} %bitcast.core_ref, bf16[16,136,128]{2,1,0:T(8,128)(2,1)S(1)} %bitcast.17, bf16[4096,512]{1,0:T(8,128)(2,1)} %own_ref.1, bf16[4096,512]{1,0:T(8,128)(2,1)} %collective-permute-done.other_ref, f32[512,512]{1,0:T(8,128)S(1)} %fusion.1.early_ref), custom_call_target="tpu_custom_call" | custom-call | flops 4294967296 | bytes 12582912 | tf_op jit(solution)/shard_map/project/pallas_call | solution.py:195
  35.0 0.1 multiply_convert_fusion
  35.1 16.3 %all_to_all.20 = f16[16,32,512]{2,1,0:T(8,128)(2,1)S(1)} all-to-all(f16[16,32,512]{2,1,0:T(8,128)(2,1)S(1)} %bitcast.21), channel_id=1, replica_groups=mesh['zh'=2,'x'=4,'c'=2,'zl'=4,'y'=4] {'y','x'}, dimensions={0} | all-to-all | bytes 1048576 | tf_op jit(solution)/shard_map/all_to_all | solution.py:218
  51.4 0.1 convert_reduce_fusion
  51.6 14.3 %all_to_all.21 = f16[8,32,512]{2,1,0:T(8,128)(2,1)S(1)} all-to-all(f16[8,32,512]{2,1,0:T(8,128)(2,1)S(1)} %broadcast_in_dim.4), channel_id=1, replica_groups=mesh['zh'=2,'x'=4,'c'=2,'zl'=4,'y'=4] {'zl','zh'}, dimensions={0} | all-to-all | bytes 524288 | tf_op jit(solution)/shard_map/all_to_all | solution.py:221
  65.9 12.0 %all_to_all.22 = f16[16,32,512]{2,1,0:T(8,128)(2,1)S(1)} all-to-all(f16[16,32,512]{2,1,0:T(8,128)(2,1)S(1)} %broadcast_in_dim.5), channel_id=1, replica_groups=mesh['zh'=2,'x'=4,'c'=2,'zl'=4,'y'=4] {'y','x'}, dimensions={0} | all-to-all | bytes 1048576 | tf_op jit(solution)/shard_map/all_to_all | solution.py:224
  78.0 0.1 convert_multiply_fusion
  78.1 1.0 %fusion = f32[512,512]{1,0:T(8,128)S(1)} fusion(f32[512,512]{1,0:T(8,128)S(1)} %bitcast.18, f32[512,512]{1,0:T(8,128)S(1)} %copy-done), kind=kOutput, calls=%fused_computation.1 | convolution fusion | flops 805830656 | bytes 3145728 | tf_op jit(solution)/shard_map/dot_general | solution.py:227
  79.1 0.6 fusion.3.made_b
  79.7 0.6 fusion.5.made_a
  80.4 5.8 %collective-permute-start.1 = (f32[256,512]{1,0:T(8,128)S(1)}, f32[256,512]{1,0:T(8,128)S(1)}, u32[]{:S(2)}, u32[]{:S(2)}) collective-permute-start(f32[256,512]{1,0:T(8,128)S(1)} %fusion.5.made_a), channel_id=1, source_target_pairs={{0,16},{16,0},{1,17},{17,1},{2,18},{18,2},{3,19},{19,3},{4,20},{20... | collective-permute-start | bytes 1572872 | tf_op jit(solution)/shard_map/ppermute | solution.py:233
  86.2 0.1 collective-permute-start.2
  86.3 1.4 %collective-permute-done.1.got_a = f32[256,512]{1,0:T(8,128)S(1)} collective-permute-done((f32[256,512]{1,0:T(8,128)S(1)}, f32[256,512]{1,0:T(8,128)S(1)}, u32[]{:S(2)}, u32[]{:S(2)}) %collective-permute-start.1) | collective-permute-done | bytes 524320 | tf_op jit(solution)/shard_map/ppermute | solution.py:233
  87.7 0.7 collective-permute-done.2.got_b
  88.4 1.1 %combine.1 = f32[512,512]{1,0:T(8,128)} custom-call(f32[256,512]{1,0:T(8,128)S(1)} %fusion.5.made_a, f32[256,512]{1,0:T(8,128)S(1)} %collective-permute-done.1.got_a, f32[256,512]{1,0:T(8,128)S(1)} %fusion.3.made_b, f32[256,512]{1,0:T(8,128)S(1)} %collective-permute-done.2.got_b, f32[512,512]{1,0:T(8,128)S(1)} %fusion.1.early_ref), custom_call_target="tpu_custom_call" | custom-call | tf_op jit(solution)/shard_map/combine/pallas_call | solution.py:234
  (5 shorter events, 0.1 us)
Async XLA Ops:
  0.0 14.7 %copy-start = (f32[512,512]{1,0:T(8,128)S(1)}, f32[512,512]{1,0:T(8,128)}, u32[]{:S(2)}) copy-start(f32[512,512]{1,0:T(8,128)} %param.9) | copy-start | bytes 3145732
  0.0 28.2 %collective-permute-start = (bf16[4096,512]{1,0:T(8,128)(2,1)}, bf16[4096,512]{1,0:T(8,128)(2,1)}, u32[]{:S(2)}, u32[]{:S(2)}) collective-permute-start(bf16[4096,512]{1,0:T(8,128)(2,1)} %own_ref.1), channel_id=1, source_target_pairs={{0,16},{16,0},{1,17},{17,1},{2,18},{18,2},{3,19},{19,3},{4,20},{20... | collective-permute-start | bytes 12582920 | tf_op jit(solution)/shard_map/ppermute | solution.py:169
  5.3 22.8 %all-to-all-start = ((bf16[16,34,4,128]{3,2,1,0:T(4,128)(2,1)}), bf16[16,34,4,128]{3,2,1,0:T(4,128)(2,1)S(1)}, u32[]{:S(2)}, u32[]{:S(2)}) async-start(bf16[16,34,4,128]{3,2,1,0:T(4,128)(2,1)} %pack.1), calls=%async_computation | async-start | bytes 1114112 | tf_op jit(solution)/shard_map/all_to_all | solution.py:188
  80.4 7.3 %collective-permute-start.1 = (f32[256,512]{1,0:T(8,128)S(1)}, f32[256,512]{1,0:T(8,128)S(1)}, u32[]{:S(2)}, u32[]{:S(2)}) collective-permute-start(f32[256,512]{1,0:T(8,128)S(1)} %fusion.5.made_a), channel_id=1, source_target_pairs={{0,16},{16,0},{1,17},{17,1},{2,18},{18,2},{3,19},{19,3},{4,20},{20... | collective-permute-start | bytes 1572872 | tf_op jit(solution)/shard_map/ppermute | solution.py:233
  86.2 2.3 %collective-permute-start.2 = (f32[256,512]{1,0:T(8,128)S(1)}, f32[256,512]{1,0:T(8,128)S(1)}, u32[]{:S(2)}, u32[]{:S(2)}) collective-permute-start(f32[256,512]{1,0:T(8,128)S(1)} %fusion.3.made_b), channel_id=1, source_target_pairs={{0,16},{16,0},{1,17},{17,1},{2,18},{18,2},{3,19},{19,3},{4,20},{20... | collective-permute-start | bytes 1572872 | tf_op jit(solution)/shard_map/ppermute | solution.py:233
